TPU v7x, 32 devices: a whole 2x2x4 slice. The times are simulated.
32 devices in a mesh: gx: 8 (over y, x, core), gy: 4 (over z).
Axes of the slice: x: 2, y: 2, z: 4, core: 2. Of those that a mesh axis runs over, the one named last changes fastest.
Arguments:
- tokens: bfloat16 [256, 16384], P('gy', 'gx'), may hold values from -6 to 6
- gate_weight: bfloat16 [16384, 26624], P('gx', 'gy'), may hold values from -0.046875 to 0.046875
- up_weight: bfloat16 [16384, 26624], P('gx', 'gy'), may hold values from -0.046875 to 0.046875
- down_weight: bfloat16 [26624, 16384], P('gy', 'gx'), may hold values from -0.0390625 to 0.0390625
Outputs:
- layer_out: bfloat16 [256, 16384], P('gy', 'gx')
All inputs are finite; a program needn't handle non-finite values.
Results may differ from a plain program's by a relative error of at most 0.0049.
Values may be sent and summed in bfloat16 or wider, within the bound.
No kernel may reach another device: no remote copies, remote signals or barrier semaphores. Data moves between devices by JAX's collectives and lax.ppermute only.
A program may use at most 192 MiB of HBM per device.

v0:
```python
import jax
import jax.numpy as jnp
from jax import lax
from jax.sharding import PartitionSpec as P


def on_device(tokens, gate_weight, up_weight, down_weight):
    feats = lax.all_gather(tokens, "gy", axis=0, tiled=True)
    gate_part = jnp.dot(feats, gate_weight, preferred_element_type=jnp.float32)
    up_part = jnp.dot(feats, up_weight, preferred_element_type=jnp.float32)
    terms = jnp.stack((gate_part, up_part), axis=0)
    summed = lax.psum_scatter(terms, "gx", scatter_dimension=1, tiled=True)
    gate, up = (summed[0], summed[1])
    hidden = (jax.nn.silu(gate) * up).astype(jnp.bfloat16)
    partial_out = jnp.dot(
        lax.all_gather(hidden, "gx", axis=0, tiled=True),
        down_weight,
        preferred_element_type=jnp.float32,
    )
    return lax.psum_scatter(partial_out, "gy", scatter_dimension=0, tiled=True).astype(jnp.bfloat16)


def solution(mesh):
    return jax.shard_map(
        on_device,
        mesh=mesh,
        in_specs=(P("gy", "gx"), P("gx", "gy"), P("gx", "gy"), P("gy", "gx")),
        out_specs=P("gy", "gx"),
        check_vma=False,
    )
```

profile of v0, /device:TPU:0, one launch (start us, length us, event | category | flops | bytes accessed | tf_op | source)
XLA Modules:
  0.0 282.7 jit_solution(7280051073648145812)
XLA Ops:
  6.5 0.0 all-gather.3.cloned.1.call-start
  6.5 0.7 all-gather.3.cloned.1.call-update
  7.3 0.0 reduce-scatter.3.cloned.1.call-start
  7.3 32.3 %all-gather.3.cloned.1.call-done = bf16[256,2048]{1,0:T(8,128)(2,1)} async-done(((bf16[64,2048]{1,0:T(8,128)(2,1)}), bf16[256,2048]{1,0:T(8,128)(2,1)}) %all-gather.3.cloned.1.call-update) | async-done | bytes 1048592 | tf_op jit(solution)/shard_map/all_gather | solution.py:8
  39.6 0.0 copy-start
  39.6 18.0 %convolution_bitcast_fusion = f32[1,256,6656]{2,1,0:T(8,128)} fusion(bf16[256,2048]{1,0:T(8,128)(2,1)} %all-gather.3.cloned.1.call-done, bf16[2048,6656]{1,0:T(8,128)(2,1)} %param.6), kind=kOutput, calls=%fused_computation.1 | convolution fusion | flops 6979321856 | bytes 35127296 | tf_op jit(solution)/shard_map/dot_general | solution.py:10
  57.6 0.0 copy-done
  57.6 15.3 %convolution_bitcast_fusion.1 = f32[1,256,6656]{2,1,0:T(8,128)} fusion(bf16[256,2048]{1,0:T(8,128)(2,1)S(1)} %copy-done, bf16[2048,6656]{1,0:T(8,128)(2,1)} %param.5), kind=kOutput, calls=%fused_computation.2 | convolution fusion | flops 6979321856 | bytes 35127296 | tf_op jit(solution)/shard_map/dot_general | solution.py:9
  72.9 10.6 %pad_maximum_fusion = f32[2,256,6656]{2,1,0:T(8,128)} fusion(f32[1,256,6656]{2,1,0:T(8,128)} %convolution_bitcast_fusion, f32[1,256,6656]{2,1,0:T(8,128)} %convolution_bitcast_fusion.1), kind=kLoop, calls=%fused_computation | loop fusion | flops 3407872 | bytes 27262976 | tf_op jit(solution)/shard_map/stack | solution.py:11
  83.5 0.0 reduce-scatter.3.cloned.1.call-update
  83.6 0.0 all-gather.5.cloned.1.call-start
  83.6 96.8 %reduce-scatter.3.cloned.1.call-done = f32[2,32,6656]{2,1,0:T(8,128)} async-done(((f32[2,256,6656]{2,1,0:T(8,128)}), f32[2,32,6656]{2,1,0:T(8,128)}) %reduce-scatter.3.cloned.1.call-update) | async-done | bytes 1703952 | tf_op jit(solution)/shard_map/reduce_scatter | solution.py:12
  180.4 2.4 fusion.1
  182.8 0.0 all-gather.5.cloned.1.call-update
  182.8 0.0 reduce-scatter.5.cloned.1.call-start
  182.8 33.4 %all-gather.5.cloned.1.call-done = bf16[256,6656]{1,0:T(8,128)(2,1)} async-done(((bf16[32,6656]{1,0:T(8,128)(2,1)}), bf16[256,6656]{1,0:T(8,128)(2,1)}) %all-gather.5.cloned.1.call-update) | async-done | bytes 3407888 | tf_op jit(solution)/shard_map/all_gather | solution.py:16
  216.2 14.4 %fusion.2 = f32[256,2048]{1,0:T(8,128)} fusion(bf16[256,6656]{1,0:T(8,128)(2,1)} %all-gather.5.cloned.1.call-done, bf16[6656,2048]{1,0:T(8,128)(2,1)} %param.7), kind=kOutput, calls=%fused_computation.7 | convolution fusion | flops 6979321856 | bytes 32768000 | tf_op jit(solution)/shard_map/dot_general | solution.py:15
  230.6 0.0 reduce-scatter.5.cloned.1.call-update
  230.6 43.8 %reduce-scatter.5.cloned.1.call-done = f32[64,2048]{1,0:T(8,128)} async-done(((f32[256,2048]{1,0:T(8,128)}), f32[64,2048]{1,0:T(8,128)}) %reduce-scatter.5.cloned.1.call-update) | async-done | bytes 524304 | tf_op jit(solution)/shard_map/reduce_scatter | solution.py:20
  274.4 1.8 convert_element_type.7
Async XLA Ops:
  6.5 33.1 %all-gather.3.cloned.1.call-start = ((), (), s32[]{:S(2)}) async-start(), calls=%async_computation.2 | async-start | bytes 1310720 | tf_op jit(solution)/shard_map/all_gather | solution.py:8
  7.3 173.1 %reduce-scatter.3.cloned.1.call-start = ((), (), s32[]{:S(2)}) async-start(), calls=%async_computation.3 | async-start | bytes 15335424 | tf_op jit(solution)/shard_map/reduce_scatter | solution.py:12
  39.6 18.0 %copy-start = (bf16[256,2048]{1,0:T(8,128)(2,1)S(1)}, bf16[256,2048]{1,0:T(8,128)(2,1)}, u32[]{:S(2)}) copy-start(bf16[256,2048]{1,0:T(8,128)(2,1)} %all-gather.3.cloned.1.call-done) | copy-start | bytes 3145732
  83.6 132.7 %all-gather.5.cloned.1.call-start = ((), (), s32[]{:S(2)}) async-start(), calls=%async_computation.4 | async-start | bytes 3833856 | tf_op jit(solution)/shard_map/all_gather | solution.py:16
  182.8 91.6 %reduce-scatter.5.cloned.1.call-start = ((), (), s32[]{:S(2)}) async-start(), calls=%async_computation.5 | async-start | bytes 2621440 | tf_op jit(solution)/shard_map/reduce_scatter | solution.py:20
Sparse Core Ops, SparseCore 0:
  8.9 30.6 all-gather.2
  83.7 96.6 reduce-scatter.2
  182.9 33.2 all-gather.4
  230.8 43.6 reduce-scatter.4
where the time goes:
time: 283 us
  waiting for transfers between devices  207 us (73%)
  matrix products  47.7 us (17%)
  other arithmetic  14.8 us (5%)
  between operations  13.1 us (5%)
    reduce_scatter x1, waiting for transfers between devices, on_device(): summed = lax.psum_scatter(terms, 'gx', scatter_dimension=1, tiled=True)  96.8 us
    reduce_scatter x1, waiting for transfers between devices, on_device(): lax.psum_scatter(partial_out, 'gy', scatter_dimension=0, tiled=True)  43.8 us
    all_gather x1, waiting for transfers between devices, on_device(): lax.all_gather(hidden, 'gx', axis=0, tiled=True)  33.4 us
    all_gather x1, waiting for transfers between devices, on_device(): feats = lax.all_gather(tokens, 'gy', axis=0, tiled=True)  32.3 us
    dot_general x1, matrix products, on_device(): up_part = jnp.dot(feats, up_weight, preferred_element_type=jnp.float32)  18 us
    dot_general x1, matrix products, on_device(): gate_part = jnp.dot(feats, gate_weight, preferred_element_type=jnp.float32)  15.3 us
    dot_general x1, matrix products, on_device(): jnp.dot(lax.all_gather(hidden, 'gx', axis=0, tiled=True), down_weight, pr...  14.4 us
    another operation x1, other arithmetic, on_device(): terms = jnp.stack((gate_part, up_part), axis=0)  10.6 us
  transfers between devices with their start and end apart: 4, of which 4 were waited for; matrix products, arithmetic and copies ran while one was open for 0% of the time, Pallas kernels for 0%

commit v1 on v0

v1 whole, which is shorter than its diff:
```python
import jax
import jax.numpy as jnp
from jax import lax
from jax.experimental import pallas as pl
from jax.experimental.pallas import tpu as pltpu
from jax.sharding import PartitionSpec as P

F32 = jnp.float32
BF16 = jnp.bfloat16
PIECES = (4, 4, 5)
HELD = ((0, 0), (0, 1), (1, 0), (1, 1))


def params(mib):
    return pltpu.CompilerParams(vmem_limit_bytes=mib << 20)


def cost(m, k, n):
    return pl.CostEstimate(flops=2 * m * k * n, transcendentals=0, bytes_accessed=2 * (m * k + k * n) + 4 * m * n)


def widths(units):
    total, ends, run = sum(PIECES), [0], 0
    for piece in PIECES:
        run += piece
        ends.append(round(units * run / total))
    return [(a, b) for a, b in zip(ends, ends[1:]) if b > a]


def block_of(size):
    return next(b for b in (512, 256, 128) if size % b == 0)


def row_blocks(groups):
    chips = groups // 2
    return [(h, 2 * q + core) for core in range(2) for h in range(2) for q in range(chips)]


def place_rows(me, parts, groups):
    rows = sum(p.shape[0] for p in parts)
    cols = parts[0].shape[1]
    step = rows // (2 * groups)

    def kernel(me_ref, *refs):
        ins, out, buf = refs[:-2], refs[-2], refs[-1]
        at = 0
        for r in ins:
            buf[at : at + r.shape[0], :] = r[...]
            at += r.shape[0]
        for i, (h, p) in enumerate(row_blocks(groups)):
            src = pl.multiple_of((h * groups + (me_ref[0] ^ p)) * step, step)
            out[i * step : (i + 1) * step, :] = buf[pl.ds(src, step), :]

    whole = lambda a: pl.BlockSpec(a.shape, lambda i, m: (0, 0))
    return pl.pallas_call(
        kernel,
        grid_spec=pltpu.PrefetchScalarGridSpec(
            num_scalar_prefetch=1,
            grid=(1,),
            in_specs=[whole(p) for p in parts],
            out_specs=pl.BlockSpec((rows, cols), lambda i, m: (0, 0)),
            scratch_shapes=[pltpu.VMEM((rows, cols), BF16)],
        ),
        out_shape=jax.ShapeDtypeStruct((rows, cols), BF16),
        compiler_params=params(4),
    )(me, *parts)


def fetch(weights, chunks, bn):
    k = weights[0].shape[0]
    shapes = [pltpu.VMEM((k, (last - first) * bn), BF16) for _, first, last in chunks]
    count = len(chunks)

    def kernel(*refs):
        ins, outs, sems = refs[: len(weights)], refs[len(weights) : -1], refs[-1]
        copies = []
        for i, (which, first, last) in enumerate(chunks):
            cols = pl.ds(first * bn, (last - first) * bn)
            copies.append(pltpu.make_async_copy(ins[which].at[:, cols], outs[i], sems.at[i]))
        for c in copies:
            c.start()
        for c in copies:
            c.wait()

    return pl.pallas_call(
        kernel,
        in_specs=[pl.BlockSpec(memory_space=pl.ANY)] * len(weights),
        out_specs=[pl.BlockSpec(memory_space=pltpu.VMEM)] * count,
        out_shape=shapes,
        scratch_shapes=[pltpu.SemaphoreType.DMA((count,))],
        compiler_params=params(1),
        cost_estimate=pl.CostEstimate(flops=0, transcendentals=0, bytes_accessed=4 * weights[0].size),
    )(*weights)


def gate_up(feats, pair, held, first, last, bn):
    rows, k = feats.shape
    half, n = rows // 2, last - first

    def kernel(x, g, u, keep, send):
        cols = pl.ds(pl.multiple_of(pl.program_id(0) * bn, bn), bn)
        for i, w in enumerate((g, u)):
            tile = w[:, cols] if held[i] else w[...]
            part = jnp.dot(x[...], tile, preferred_element_type=F32)
            keep[i] = part[:half]
            send[i] = part[half:].astype(BF16)

    o_spec = pl.BlockSpec((2, half, bn), lambda j: (0, 0, j))
    stream = pl.BlockSpec((k, bn), lambda j: (0, first + j))
    return pl.pallas_call(
        kernel,
        grid=(n,),
        in_specs=[pl.BlockSpec((rows, k), lambda j: (0, 0))]
        + [pl.BlockSpec(memory_space=pltpu.VMEM) if h else stream for h in held],
        out_specs=[o_spec, o_spec],
        out_shape=[
            jax.ShapeDtypeStruct((2, half, n * bn), F32),
            jax.ShapeDtypeStruct((2, half, n * bn), BF16),
        ],
        compiler_params=params(5 if all(held) else 45),
        cost_estimate=cost(rows, k, 2 * n * bn),
    )(feats, *pair)


def down(me, hiddens, acc, down_weight, start, groups, owners):
    w = hiddens[0].shape[1]
    rows, n = sum(h.shape[0] for h in hiddens), down_weight.shape[1]
    step = rows // (2 * groups)
    bn = block_of(n)
    count = len(hiddens)

    def kernel(me_ref, *refs):
        refs = list(refs)
        ins, wd = refs[:count], refs[count]
        prev = refs[count + 1] if acc is not None else None
        outs, lhs = refs[count + 1 + (acc is not None) : -1], refs[-1]

        @pl.when(pl.program_id(0) == 0)
        def _():
            per = len(row_blocks(groups)) // count
            for i, (h, p) in enumerate(row_blocks(groups)):
                at = (i % per) * step
                dst = pl.multiple_of((h * groups + (me_ref[0] ^ p)) * step, step)
                lhs[pl.ds(dst, step), :] = ins[i // per][at : at + step, :]

        total = jnp.dot(lhs[...], wd[...], preferred_element_type=F32)
        if prev is not None:
            total = total + prev[...]
        each = rows // len(outs)
        for s, o in enumerate(outs):
            o[...] = total[s * each : (s + 1) * each].astype(o.dtype)

    in_specs = [pl.BlockSpec(h.shape, lambda j, m: (0, 0)) for h in hiddens]
    in_specs.append(pl.BlockSpec((pl.Element(w), pl.Element(bn)), lambda j, m: (start, j * bn)))
    args = [*hiddens, down_weight]
    if acc is not None:
        in_specs.append(pl.BlockSpec((rows, bn), lambda j, m: (0, j)))
        args.append(acc)
    each = rows // owners
    out_shape = [jax.ShapeDtypeStruct((each, n), F32 if s == 0 else BF16) for s in range(owners)]
    return pl.pallas_call(
        kernel,
        grid_spec=pltpu.PrefetchScalarGridSpec(
            num_scalar_prefetch=1,
            grid=(n // bn,),
            in_specs=in_specs,
            out_specs=[pl.BlockSpec((each, bn), lambda j, m: (0, j))] * owners,
            scratch_shapes=[pltpu.VMEM((rows, w), BF16)],
        ),
        out_shape=out_shape,
        compiler_params=params(40),
        cost_estimate=cost(rows, w, n),
    )(me, *args)


def make(nx, nz):
    def swap(v, mask):
        return lax.ppermute(v, "gx", [(i, i ^ mask) for i in range(nx)])

    def shift(v, s):
        return lax.ppermute(v, "gy", [(i, (i + s) % nz) for i in range(nz)])

    chips = nx // 2
    bits = chips.bit_length() - 1

    def layer(tokens, gate_weight, up_weight, down_weight):
        me = lax.axis_index("gx").astype(jnp.int32).reshape(1)
        parts = [tokens] + [shift(tokens, s) for s in range(1, nz)]
        feats = place_rows(me, parts, nx)
        hid = gate_weight.shape[1]
        bn = block_of(hid)
        chunks = widths(hid // bn)
        both = (gate_weight, up_weight)
        early = [(i, *chunks[c]) for c, i in HELD]
        got = fetch(both, early, bn)
        weights = [list(both) for _ in chunks]
        for (c, i), v in zip(HELD, got):
            weights[c][i] = v
        own = feats.shape[0] // (2 * nx)
        acc = None
        for c, (first, last) in enumerate(chunks):
            keep, send = gate_up(feats, weights[c], [(c, i) in HELD for i in range(2)], first, last, bn)
            got = swap(send, 1)
            halves = []
            for h in range(2):
                order = range(bits) if h == 0 else range(bits)[::-1]
                rows = slice(h * chips * own, (h + 1) * chips * own)
                block = keep[:, rows] + got[:, rows].astype(F32)
                for i, b in enumerate(order):
                    wide = block.reshape(2, -1, 2, block.shape[1] // 2 ** (1 + sum(1 for o in order[i + 1 :] if o > b)), block.shape[2])
                    stay, go = wide[:, :, 0], wide[:, :, 1].astype(BF16)
                    flat = (2, block.shape[1] // 2, block.shape[2])
                    come = swap(go.reshape(flat), 2 << b)
                    block = stay.reshape(flat) + come.astype(F32)
                hidden = (jax.nn.silu(block[0]) * block[1]).astype(BF16)
                for i, b in reversed(list(enumerate(order))):
                    come = swap(hidden, 2 << b)
                    inner = own * 2 ** sum(1 for o in order[i + 1 :] if o < b)
                    both = [v.reshape(-1, 1, inner, v.shape[1]) for v in (hidden, come)]
                    hidden = jnp.concatenate(both, axis=1).reshape(-1, hidden.shape[1])
                halves.append(hidden)
            halves += [swap(v, 1) for v in halves]
            final = c == len(chunks) - 1
            acc = down(me, halves, acc, down_weight, first * bn, nx, nz if final else 1)
            acc = acc if final else acc[0]
        out = acc[0]
        for s in range(1, nz):
            out = out + shift(acc[s], -s).astype(F32)
        return out.astype(BF16)

    return layer


def solution(mesh):
    return jax.shard_map(
        make(mesh.shape["gx"], mesh.shape["gy"]),
        mesh=mesh,
        in_specs=(P("gy", "gx"), P("gx", "gy"), P("gx", "gy"), P("gy", "gx")),
        out_specs=P("gy", "gx"),
        check_vma=False,
    )
```

time: 283 us -> 171 us (0.60)
  waiting for transfers between devices: 207 us -> 73 us
  Pallas kernels: 0 us -> 50 us
  matrix products: 47.7 us -> 0 us
  starting transfers between devices: 0.12 us -> 43.9 us
  between operations: 13.1 us -> 0.55 us
  other arithmetic: 14.8 us -> 3.13 us
    reduce_scatter x2 -> x0, waiting for transfers between devices: 141 us -> none  [the longest x1 96.8 us: on_device(): summed = lax.psum_scatter(terms, 'gx', scatter_dimension=1, tiled=True)]
    ppermute x0 -> x39, waiting for transfers between devices: none -> 73 us  [the longest x33 44.8 us: swap(): return lax.ppermute(v, 'gx', [(i, i ^ mask) for i in range(nx)])]
    all_gather x2 -> x0, waiting for transfers between devices: 65.7 us -> none  [the longest x1 33.4 us: on_device(): lax.all_gather(hidden, 'gx', axis=0, tiled=True)]
    pallas_call x0 -> x8, Pallas kernels: none -> 50 us  [the longest x3 21.2 us: gate_up(): pl.pallas_call(kernel, grid=(n,), in_specs=[pl.BlockSpec((rows, k), lambd...]
    dot_general x3 -> x0, matrix products: 47.7 us -> none  [the longest x1 18 us: on_device(): up_part = jnp.dot(feats, up_weight, preferred_element_type=jnp.float32)]
    ppermute x0 -> x39, starting transfers between devices: none -> 43.9 us  [the longest x33 29.1 us: swap(): return lax.ppermute(v, 'gx', [(i, i ^ mask) for i in range(nx)])]
    another operation x1 -> x3, other arithmetic: 10.6 us -> 0.06 us  [layer(): both = [v.reshape(-1, 1, inner, v.shape[1]) for v in (hidden, come)]]
  transfers between devices with their start and end apart: 4 -> 39, of which waited for: 4 -> 18; matrix products, arithmetic and copies ran while one was open for 0% -> 2% of each run, Pallas kernels for 0% -> 22%
where the time goes in v1:
time: 171 us
  waiting for transfers between devices  73 us (43%)
  Pallas kernels  50 us (29%)
  starting transfers between devices  43.9 us (26%)
  other arithmetic  3.13 us (2%)
    ppermute x33, waiting for transfers between devices, swap(): return lax.ppermute(v, 'gx', [(i, i ^ mask) for i in range(nx)])  44.8 us
    ppermute x33, starting transfers between devices, swap(): return lax.ppermute(v, 'gx', [(i, i ^ mask) for i in range(nx)])  29.1 us
    ppermute x6, waiting for transfers between devices, shift(): return lax.ppermute(v, 'gy', [(i, (i + s) % nz) for i in range(nz)])  28.2 us
    pallas_call x3, Pallas kernels, gate_up(): pl.pallas_call(kernel, grid=(n,), in_specs=[pl.BlockSpec((rows, k), lambd...  21.2 us
    pallas_call x3, Pallas kernels, down(): pl.pallas_call(kernel, grid_spec=pltpu.PrefetchScalarGridSpec(num_scalar_...  18 us
    ppermute x6, starting transfers between devices, shift(): return lax.ppermute(v, 'gy', [(i, (i + s) % nz) for i in range(nz)])  14.8 us
    pallas_call x1, Pallas kernels, fetch(): pl.pallas_call(kernel, in_specs=[pl.BlockSpec(memory_space=pl.ANY)] * len...  10.7 us
  transfers between devices with their start and end apart: 39, of which 18 were waited for; matrix products, arithmetic and copies ran while one was open for 2% of the time, Pallas kernels for 22%

profile of v1, /device:TPU:0, one launch (start us, length us, event | category | flops | bytes accessed | tf_op | source)
XLA Modules:
  0.0 171.0 jit_solution(2209128331851893320)
XLA Ops:
  0.0 3.1 %collective-permute-start = (bf16[64,2048]{1,0:T(8,128)(2,1)}, bf16[64,2048]{1,0:T(8,128)(2,1)S(1)}, u32[]{:S(2)}, u32[]{:S(2)}) collective-permute-start(bf16[64,2048]{1,0:T(8,128)(2,1)} %refs_0_.2), channel_id=1, source_target_pairs={{0,1},{1,2},{2,3},{3,0},{4,5},{5,6},{6,7},{7,4},{8,9},{9,10},{10,1... | collective-permute-start | bytes 786440 | tf_op jit(solution)/shard_map/ppermute | solution.py:181
  3.1 2.6 %collective-permute-start.1 = (bf16[64,2048]{1,0:T(8,128)(2,1)}, bf16[64,2048]{1,0:T(8,128)(2,1)S(1)}, u32[]{:S(2)}, u32[]{:S(2)}) collective-permute-start(bf16[64,2048]{1,0:T(8,128)(2,1)} %refs_0_.2), channel_id=1, source_target_pairs={{0,2},{1,3},{2,0},{3,1},{4,6},{5,7},{6,4},{7,5},{8,10},{9,11},{10,... | collective-permute-start | bytes 786440 | tf_op jit(solution)/shard_map/ppermute | solution.py:181
  7.0 10.7 %shard_map.48 = (bf16[2048,2048]{1,0:T(8,128)(2,1)S(1)}, bf16[2048,2048]{1,0:T(8,128)(2,1)S(1)}, bf16[2048,2048]{1,0:T(8,128)(2,1)S(1)}, bf16[2048,2048]{1,0:T(8,128)(2,1)S(1)}) custom-call(bf16[2048,6656]{1,0:T(8,128)(2,1)} %refs_0_.3, bf16[2048,6656]{1,0:T(8,128)(2,1)} %refs_1_.1), custom_call_target="tpu_custom_call" | custom-call | bytes 54525952 | tf_op jit(solution)/shard_map/pallas_call | solution.py:85
  17.7 5.3 %collective-permute-done.1.refs_2_ = bf16[64,2048]{1,0:T(8,128)(2,1)S(1)} collective-permute-done((bf16[64,2048]{1,0:T(8,128)(2,1)}, bf16[64,2048]{1,0:T(8,128)(2,1)S(1)}, u32[]{:S(2)}, u32[]{:S(2)}) %collective-permute-start.1) | collective-permute-done | bytes 262176 | tf_op jit(solution)/shard_map/ppermute | solution.py:181
  23.1 5.3 %shard_map.50 = (f32[2,128,2048]{2,1,0:T(8,128)S(1)}, bf16[2,128,2048]{2,1,0:T(8,128)(2,1)S(1)}) custom-call(bf16[256,2048]{1,0:T(8,128)(2,1)S(1)} %shard_map.46.x, bf16[2048,2048]{1,0:T(8,128)(2,1)S(1)} %get-tuple-element.25.g, bf16[2048,2048]{1,0:T(8,128)(2,1)S(1)} %get-tuple-element.26.u), custom_call_target="tpu_custom_call" | custom-call | flops 4294967296 | bytes 22020096 | tf_op jit(solution)/shard_map/pallas_call | solution.py:110
  28.5 5.2 %shard_map.49 = (f32[2,128,2048]{2,1,0:T(8,128)S(1)}, bf16[2,128,2048]{2,1,0:T(8,128)(2,1)S(1)}) custom-call(bf16[256,2048]{1,0:T(8,128)(2,1)S(1)} %shard_map.46.x, bf16[2048,2048]{1,0:T(8,128)(2,1)S(1)} %get-tuple-element.21.g, bf16[2048,2048]{1,0:T(8,128)(2,1)S(1)} %get-tuple-element.22.u), custom_call_target="tpu_custom_call" | custom-call | flops 4294967296 | bytes 22020096 | tf_op jit(solution)/shard_map/pallas_call | solution.py:110
  34.3 10.7 %shard_map.47 = (f32[2,128,2560]{2,1,0:T(8,128)S(1)}, bf16[2,128,2560]{2,1,0:T(8,128)(2,1)S(1)}) custom-call(bf16[256,2048]{1,0:T(8,128)(2,1)S(1)} %shard_map.46.x, bf16[2048,6656]{1,0:T(8,128)(2,1)} %refs_0_.3, bf16[2048,6656]{1,0:T(8,128)(2,1)} %refs_1_.1), custom_call_target="tpu_custom_call" | custom-call | flops 5368709120 | bytes 27262976 | tf_op jit(solution)/shard_map/pallas_call | solution.py:110
  45.8 1.6 collective-permute-start.30
  50.5 4.6 %collective-permute-done.30 = bf16[2,32,2048]{2,1,0:T(8,128)(2,1)S(1)} collective-permute-done((bf16[2,32,2048]{2,1,0:T(8,128)(2,1)S(1)}, bf16[2,32,2048]{2,1,0:T(8,128)(2,1)S(1)}, u32[]{:S(2)}, u32[]{:S(2)}) %collective-permute-start.30) | collective-permute-done | bytes 262176 | tf_op jit(solution)/shard_map/ppermute | solution.py:178
  55.1 1.6 collective-permute-start.31
  56.8 1.6 collective-permute-start.27
  58.3 2.3 %collective-permute-done.19 = bf16[2,32,2048]{2,1,0:T(8,128)(2,1)S(1)} collective-permute-done((bf16[2,32,2048]{2,1,0:T(8,128)(2,1)S(1)}, bf16[2,32,2048]{2,1,0:T(8,128)(2,1)S(1)}, u32[]{:S(2)}, u32[]{:S(2)}) %collective-permute-start.19) | collective-permute-done | bytes 262176 | tf_op jit(solution)/shard_map/ppermute | solution.py:178
  60.7 1.6 collective-permute-start.20
  62.4 1.6 collective-permute-start.16
  67.9 1.6 collective-permute-start.32
  71.1 5.1 %collective-permute-done.32 = bf16[16,2048]{1,0:T(8,128)(2,1)S(1)} collective-permute-done((bf16[16,2048]{1,0:T(8,128)(2,1)S(1)}, bf16[16,2048]{1,0:T(8,128)(2,1)S(1)}, u32[]{:S(2)}, u32[]{:S(2)}) %collective-permute-start.32) | collective-permute-done | bytes 65568 | tf_op jit(solution)/shard_map/ppermute | solution.py:178
  76.7 1.6 collective-permute-start.33
  78.3 1.6 collective-permute-start.29
  81.7 1.6 collective-permute-done.33
  86.1 2.1 %collective-permute-done.18 = bf16[32,2048]{1,0:T(8,128)(2,1)S(1)} collective-permute-done((bf16[32,2048]{1,0:T(8,128)(2,1)S(1)}, bf16[32,2048]{1,0:T(8,128)(2,1)S(1)}, u32[]{:S(2)}, u32[]{:S(2)}) %collective-permute-start.18) | collective-permute-done | bytes 131104 | tf_op jit(solution)/shard_map/ppermute | solution.py:178
  90.6 4.5 %collective-permute-done.9 = bf16[2,16,2560]{2,1,0:T(8,128)(2,1)S(1)} collective-permute-done((bf16[2,16,2560]{2,1,0:T(8,128)(2,1)S(1)}, bf16[2,16,2560]{2,1,0:T(8,128)(2,1)S(1)}, u32[]{:S(2)}, u32[]{:S(2)}) %collective-permute-start.9) | collective-permute-done | bytes 163872 | tf_op jit(solution)/shard_map/ppermute | solution.py:178
  95.8 4.7 %collective-permute-done.5 = bf16[2,16,2560]{2,1,0:T(8,128)(2,1)S(1)} collective-permute-done((bf16[2,16,2560]{2,1,0:T(8,128)(2,1)S(1)}, bf16[2,16,2560]{2,1,0:T(8,128)(2,1)S(1)}, u32[]{:S(2)}, u32[]{:S(2)}) %collective-permute-start.5) | collective-permute-done | bytes 163872 | tf_op jit(solution)/shard_map/ppermute | solution.py:178
  102.1 2.8 %collective-permute-done.10 = bf16[16,2560]{1,0:T(8,128)(2,1)S(1)} collective-permute-done((bf16[16,2560]{1,0:T(8,128)(2,1)S(1)}, bf16[16,2560]{1,0:T(8,128)(2,1)S(1)}, u32[]{:S(2)}, u32[]{:S(2)}) %collective-permute-start.10) | collective-permute-done | bytes 81952 | tf_op jit(solution)/shard_map/ppermute | solution.py:178
  105.4 4.8 %collective-permute-done.6 = bf16[16,2560]{1,0:T(8,128)(2,1)S(1)} collective-permute-done((bf16[16,2560]{1,0:T(8,128)(2,1)S(1)}, bf16[16,2560]{1,0:T(8,128)(2,1)S(1)}, u32[]{:S(2)}, u32[]{:S(2)}) %collective-permute-start.6) | collective-permute-done | bytes 81952 | tf_op jit(solution)/shard_map/ppermute | solution.py:178
  110.7 4.8 %collective-permute-done.11 = bf16[32,2560]{1,0:T(8,128)(2,1)S(1)} collective-permute-done((bf16[32,2560]{1,0:T(8,128)(2,1)S(1)}, bf16[32,2560]{1,0:T(8,128)(2,1)S(1)}, u32[]{:S(2)}, u32[]{:S(2)}) %collective-permute-start.11) | collective-permute-done | bytes 163872 | tf_op jit(solution)/shard_map/ppermute | solution.py:178
  117.1 3.8 %collective-permute-done.7 = bf16[32,2560]{1,0:T(8,128)(2,1)S(1)} collective-permute-done((bf16[32,2560]{1,0:T(8,128)(2,1)S(1)}, bf16[32,2560]{1,0:T(8,128)(2,1)S(1)}, u32[]{:S(2)}, u32[]{:S(2)}) %collective-permute-start.7) | collective-permute-done | bytes 163872 | tf_op jit(solution)/shard_map/ppermute | solution.py:178
  121.5 5.7 %shard_map.51.refs_5_ = f32[256,2048]{1,0:T(8,128)S(1)} custom-call(s32[1]{0:T(128)} %bitcast.me_ref, bf16[64,2048]{1,0:T(8,128)(2,1)S(1)} %bitcast.324, bf16[64,2048]{1,0:T(8,128)(2,1)S(1)} %bitcast.322, bf16[64,2048]{1,0:T(8,128)(2,1)S(1)} %collective-permute-done.34.refs_2_, bf16[64,2048]{1,0:T(8,128)(2,1)S(1)} %collective-permute-done.35.refs_3_, ...), custom_call_target="tpu_custom_call" | custom-call | flops 2147483648 | bytes 11534336 | tf_op jit(solution)/shard_map/pallas_call | solution.py:161
  127.2 5.8 %shard_map.52.refs_5_ = f32[256,2048]{1,0:T(8,128)S(1)} custom-call(s32[1]{0:T(128)} %bitcast.me_ref, bf16[64,2048]{1,0:T(8,128)(2,1)S(1)} %bitcast.328, bf16[64,2048]{1,0:T(8,128)(2,1)S(1)} %bitcast.326, bf16[64,2048]{1,0:T(8,128)(2,1)S(1)} %collective-permute-done.23.refs_2_, bf16[64,2048]{1,0:T(8,128)(2,1)S(1)} %collective-permute-done.24.refs_3_, ...), custom_call_target="tpu_custom_call" | custom-call | flops 2147483648 | bytes 11534336 | tf_op jit(solution)/shard_map/pallas_call | solution.py:161
  133.0 6.5 %shard_map.53 = (f32[64,2048]{1,0:T(8,128)S(1)}, bf16[64,2048]{1,0:T(8,128)(2,1)S(1)}, bf16[64,2048]{1,0:T(8,128)(2,1)S(1)}, bf16[64,2048]{1,0:T(8,128)(2,1)S(1)}) custom-call(s32[1]{0:T(128)} %bitcast.me_ref, bf16[64,2560]{1,0:T(8,128)(2,1)S(1)} %bitcast.320, bf16[64,2560]{1,0:T(8,128)(2,1)S(1)} %bitcast.318, ...), custom_call_target="tpu_custom_call" | custom-call | flops 2684354560 | bytes 13893632 | tf_op jit(solution)/shard_map/pallas_call | solution.py:161
  139.5 7.2 %collective-permute-start.36 = (bf16[64,2048]{1,0:T(8,128)(2,1)S(1)}, bf16[64,2048]{1,0:T(8,128)(2,1)S(1)}, u32[]{:S(2)}, u32[]{:S(2)}) collective-permute-start(bf16[64,2048]{1,0:T(8,128)(2,1)S(1)} %get-tuple-element.30), channel_id=1, source_target_pairs={{0,3},{1,0},{2,1},{3,2},{4,7},{5,4},{6,5},{7,6},{8,11},{9,8},{10,9... | collective-permute-start | bytes 786440 | tf_op jit(solution)/shard_map/ppermute | solution.py:181
  147.3 6.1 %collective-permute-done.36 = bf16[64,2048]{1,0:T(8,128)(2,1)S(1)} collective-permute-done((bf16[64,2048]{1,0:T(8,128)(2,1)S(1)}, bf16[64,2048]{1,0:T(8,128)(2,1)S(1)}, u32[]{:S(2)}, u32[]{:S(2)}) %collective-permute-start.36) | collective-permute-done | bytes 262176 | tf_op jit(solution)/shard_map/ppermute | solution.py:181
  153.5 16.7 %collective-permute-done.37 = bf16[64,2048]{1,0:T(8,128)(2,1)S(1)} collective-permute-done((bf16[64,2048]{1,0:T(8,128)(2,1)S(1)}, bf16[64,2048]{1,0:T(8,128)(2,1)S(1)}, u32[]{:S(2)}, u32[]{:S(2)}) %collective-permute-start.37) | collective-permute-done | bytes 262176 | tf_op jit(solution)/shard_map/ppermute | solution.py:181
  (114 shorter events, 26.2 us)
Async XLA Ops:
  0.0 17.7 %collective-permute-start = (bf16[64,2048]{1,0:T(8,128)(2,1)}, bf16[64,2048]{1,0:T(8,128)(2,1)S(1)}, u32[]{:S(2)}, u32[]{:S(2)}) collective-permute-start(bf16[64,2048]{1,0:T(8,128)(2,1)} %refs_0_.2), channel_id=1, source_target_pairs={{0,1},{1,2},{2,3},{3,0},{4,5},{5,6},{6,7},{7,4},{8,9},{9,10},{10,1... | collective-permute-start | bytes 786440 | tf_op jit(solution)/shard_map/ppermute | solution.py:181
  3.1 19.9 %collective-permute-start.1 = (bf16[64,2048]{1,0:T(8,128)(2,1)}, bf16[64,2048]{1,0:T(8,128)(2,1)S(1)}, u32[]{:S(2)}, u32[]{:S(2)}) collective-permute-start(bf16[64,2048]{1,0:T(8,128)(2,1)} %refs_0_.2), channel_id=1, source_target_pairs={{0,2},{1,3},{2,0},{3,1},{4,6},{5,7},{6,4},{7,5},{8,10},{9,11},{10,... | collective-permute-start | bytes 786440 | tf_op jit(solution)/shard_map/ppermute | solution.py:181
  5.6 17.3 %collective-permute-start.2 = (bf16[64,2048]{1,0:T(8,128)(2,1)}, bf16[64,2048]{1,0:T(8,128)(2,1)S(1)}, u32[]{:S(2)}, u32[]{:S(2)}) collective-permute-start(bf16[64,2048]{1,0:T(8,128)(2,1)} %refs_0_.2), channel_id=1, source_target_pairs={{0,3},{1,0},{2,1},{3,2},{4,7},{5,4},{6,5},{7,6},{8,11},{9,8},{10,9... | collective-permute-start | bytes 786440 | tf_op jit(solution)/shard_map/ppermute | solution.py:181
  28.4 16.6 %collective-permute-start.25 = (bf16[2,128,2048]{2,1,0:T(8,128)(2,1)S(1)}, bf16[2,128,2048]{2,1,0:T(8,128)(2,1)S(1)}, u32[]{:S(2)}, u32[]{:S(2)}) collective-permute-start(bf16[2,128,2048]{2,1,0:T(8,128)(2,1)S(1)} %get-tuple-element.28), channel_id=1, source_target_pairs={{0,4},{4,0},{8,12},{12,8},{16,20},{20,16},{24,28},{28,24},{1,5},{5... | collective-permute-start | bytes 3145736 | tf_op jit(solution)/shard_map/ppermute | solution.py:178
  33.7 11.7 %collective-permute-start.14 = (bf16[2,128,2048]{2,1,0:T(8,128)(2,1)S(1)}, bf16[2,128,2048]{2,1,0:T(8,128)(2,1)S(1)}, u32[]{:S(2)}, u32[]{:S(2)}) collective-permute-start(bf16[2,128,2048]{2,1,0:T(8,128)(2,1)S(1)} %get-tuple-element.24), channel_id=1, source_target_pairs={{0,4},{4,0},{8,12},{12,8},{16,20},{20,16},{24,28},{28,24},{1,5},{5... | collective-permute-start | bytes 3145736 | tf_op jit(solution)/shard_map/ppermute | solution.py:178
  45.8 9.2 %collective-permute-start.30 = (bf16[2,32,2048]{2,1,0:T(8,128)(2,1)S(1)}, bf16[2,32,2048]{2,1,0:T(8,128)(2,1)S(1)}, u32[]{:S(2)}, u32[]{:S(2)}) collective-permute-start(bf16[2,32,2048]{2,1,0:T(8,128)(2,1)S(1)} %fusion.7), channel_id=1, source_target_pairs={{0,16},{4,20},{8,24},{12,28},{16,0},{20,4},{24,8},{28,12},{1,17},{... | collective-permute-start | bytes 786440 | tf_op jit(solution)/shard_map/ppermute | solution.py:178
  47.4 9.3 %collective-permute-start.26 = (bf16[2,32,2048]{2,1,0:T(8,128)(2,1)S(1)}, bf16[2,32,2048]{2,1,0:T(8,128)(2,1)S(1)}, u32[]{:S(2)}, u32[]{:S(2)}) collective-permute-start(bf16[2,32,2048]{2,1,0:T(8,128)(2,1)S(1)} %bitcast.361), channel_id=1, source_target_pairs={{0,8},{4,12},{8,0},{12,4},{16,24},{20,28},{24,16},{28,20},{1,9},{5... | collective-permute-start | bytes 786440 | tf_op jit(solution)/shard_map/ppermute | solution.py:178
  48.9 11.7 %collective-permute-start.19 = (bf16[2,32,2048]{2,1,0:T(8,128)(2,1)S(1)}, bf16[2,32,2048]{2,1,0:T(8,128)(2,1)S(1)}, u32[]{:S(2)}, u32[]{:S(2)}) collective-permute-start(bf16[2,32,2048]{2,1,0:T(8,128)(2,1)S(1)} %fusion.6), channel_id=1, source_target_pairs={{0,16},{4,20},{8,24},{12,28},{16,0},{20,4},{24,8},{28,12},{1,17},{... | collective-permute-start | bytes 786440 | tf_op jit(solution)/shard_map/ppermute | solution.py:178
  49.5 12.8 %collective-permute-start.15 = (bf16[2,32,2048]{2,1,0:T(8,128)(2,1)S(1)}, bf16[2,32,2048]{2,1,0:T(8,128)(2,1)S(1)}, u32[]{:S(2)}, u32[]{:S(2)}) collective-permute-start(bf16[2,32,2048]{2,1,0:T(8,128)(2,1)S(1)} %bitcast.360), channel_id=1, source_target_pairs={{0,8},{4,12},{8,0},{12,4},{16,24},{20,28},{24,16},{28,20},{1,9},{5... | collective-permute-start | bytes 786440 | tf_op jit(solution)/shard_map/ppermute | solution.py:178
  55.1 9.9 %collective-permute-start.31 = (bf16[2,16,2048]{2,1,0:T(8,128)(2,1)S(1)}, bf16[2,16,2048]{2,1,0:T(8,128)(2,1)S(1)}, u32[]{:S(2)}, u32[]{:S(2)}) collective-permute-start(bf16[2,16,2048]{2,1,0:T(8,128)(2,1)S(1)} %fusion.33), channel_id=1, source_target_pairs={{0,8},{4,12},{8,0},{12,4},{16,24},{20,28},{24,16},{28,20},{1,9},{5... | collective-permute-start | bytes 393224 | tf_op jit(solution)/shard_map/ppermute | solution.py:178
  56.8 9.9 %collective-permute-start.27 = (bf16[2,16,2048]{2,1,0:T(8,128)(2,1)S(1)}, bf16[2,16,2048]{2,1,0:T(8,128)(2,1)S(1)}, u32[]{:S(2)}, u32[]{:S(2)}) collective-permute-start(bf16[2,16,2048]{2,1,0:T(8,128)(2,1)S(1)} %fusion.32), channel_id=1, source_target_pairs={{0,16},{4,20},{8,24},{12,28},{16,0},{20,4},{24,8},{28,12},{1,17},{... | collective-permute-start | bytes 393224 | tf_op jit(solution)/shard_map/ppermute | solution.py:178
  60.7 7.1 %collective-permute-start.20 = (bf16[2,16,2048]{2,1,0:T(8,128)(2,1)S(1)}, bf16[2,16,2048]{2,1,0:T(8,128)(2,1)S(1)}, u32[]{:S(2)}, u32[]{:S(2)}) collective-permute-start(bf16[2,16,2048]{2,1,0:T(8,128)(2,1)S(1)} %fusion.31), channel_id=1, source_target_pairs={{0,8},{4,12},{8,0},{12,4},{16,24},{20,28},{24,16},{28,20},{1,9},{5... | collective-permute-start | bytes 393224 | tf_op jit(solution)/shard_map/ppermute | solution.py:178
  62.4 7.1 %collective-permute-start.16 = (bf16[2,16,2048]{2,1,0:T(8,128)(2,1)S(1)}, bf16[2,16,2048]{2,1,0:T(8,128)(2,1)S(1)}, u32[]{:S(2)}, u32[]{:S(2)}) collective-permute-start(bf16[2,16,2048]{2,1,0:T(8,128)(2,1)S(1)} %fusion.30), channel_id=1, source_target_pairs={{0,16},{4,20},{8,24},{12,28},{16,0},{20,4},{24,8},{28,12},{1,17},{... | collective-permute-start | bytes 393224 | tf_op jit(solution)/shard_map/ppermute | solution.py:178
  64.0 24.3 %collective-permute-start.8 = (bf16[2,32,2560]{2,1,0:T(8,128)(2,1)S(1)}, bf16[2,32,2560]{2,1,0:T(8,128)(2,1)S(1)}, u32[]{:S(2)}, u32[]{:S(2)}) collective-permute-start(bf16[2,32,2560]{2,1,0:T(8,128)(2,1)S(1)} %fusion.3), channel_id=1, source_target_pairs={{0,16},{4,20},{8,24},{12,28},{16,0},{20,4},{24,8},{28,12},{1,17},{... | collective-permute-start | bytes 983048 | tf_op jit(solution)/shard_map/ppermute | solution.py:178
  65.0 24.0 %collective-permute-start.4 = (bf16[2,32,2560]{2,1,0:T(8,128)(2,1)S(1)}, bf16[2,32,2560]{2,1,0:T(8,128)(2,1)S(1)}, u32[]{:S(2)}, u32[]{:S(2)}) collective-permute-start(bf16[2,32,2560]{2,1,0:T(8,128)(2,1)S(1)} %bitcast.359), channel_id=1, source_target_pairs={{0,8},{4,12},{8,0},{12,4},{16,24},{20,28},{24,16},{28,20},{1,9},{5... | collective-permute-start | bytes 983048 | tf_op jit(solution)/shard_map/ppermute | solution.py:178
  67.9 8.2 %collective-permute-start.32 = (bf16[16,2048]{1,0:T(8,128)(2,1)S(1)}, bf16[16,2048]{1,0:T(8,128)(2,1)S(1)}, u32[]{:S(2)}, u32[]{:S(2)}) collective-permute-start(bf16[16,2048]{1,0:T(8,128)(2,1)S(1)} %fusion.34), channel_id=1, source_target_pairs={{0,8},{4,12},{8,0},{12,4},{16,24},{20,28},{24,16},{28,20},{1,9},{5... | collective-permute-start | bytes 196616 | tf_op jit(solution)/shard_map/ppermute | solution.py:178
  69.6 7.0 %collective-permute-start.28 = (bf16[16,2048]{1,0:T(8,128)(2,1)S(1)}, bf16[16,2048]{1,0:T(8,128)(2,1)S(1)}, u32[]{:S(2)}, u32[]{:S(2)}) collective-permute-start(bf16[16,2048]{1,0:T(8,128)(2,1)S(1)} %fusion.42), channel_id=1, source_target_pairs={{0,16},{4,20},{8,24},{12,28},{16,0},{20,4},{24,8},{28,12},{1,17},{... | collective-permute-start | bytes 196616 | tf_op jit(solution)/shard_map/ppermute | solution.py:178
  70.5 7.8 %collective-permute-start.21 = (bf16[16,2048]{1,0:T(8,128)(2,1)S(1)}, bf16[16,2048]{1,0:T(8,128)(2,1)S(1)}, u32[]{:S(2)}, u32[]{:S(2)}) collective-permute-start(bf16[16,2048]{1,0:T(8,128)(2,1)S(1)} %fusion.50), channel_id=1, source_target_pairs={{0,8},{4,12},{8,0},{12,4},{16,24},{20,28},{24,16},{28,20},{1,9},{5... | collective-permute-start | bytes 196616 | tf_op jit(solution)/shard_map/ppermute | solution.py:178
  76.7 6.5 %collective-permute-start.33 = (bf16[32,2048]{1,0:T(8,128)(2,1)S(1)}, bf16[32,2048]{1,0:T(8,128)(2,1)S(1)}, u32[]{:S(2)}, u32[]{:S(2)}) collective-permute-start(bf16[32,2048]{1,0:T(8,128)(2,1)S(1)} %bitcast.355), channel_id=1, source_target_pairs={{0,16},{4,20},{8,24},{12,28},{16,0},{20,4},{24,8},{28,12},{1,17},{... | collective-permute-start | bytes 393224 | tf_op jit(solution)/shard_map/ppermute | solution.py:178
  78.3 6.4 %collective-permute-start.29 = (bf16[32,2048]{1,0:T(8,128)(2,1)S(1)}, bf16[32,2048]{1,0:T(8,128)(2,1)S(1)}, u32[]{:S(2)}, u32[]{:S(2)}) collective-permute-start(bf16[32,2048]{1,0:T(8,128)(2,1)S(1)} %bitcast.365), channel_id=1, source_target_pairs={{0,8},{4,12},{8,0},{12,4},{16,24},{20,28},{24,16},{28,20},{1,9},{5... | collective-permute-start | bytes 393224 | tf_op jit(solution)/shard_map/ppermute | solution.py:178
  84.8 36.2 %collective-permute-start.35 = (bf16[64,2048]{1,0:T(8,128)(2,1)S(1)}, bf16[64,2048]{1,0:T(8,128)(2,1)S(1)}, u32[]{:S(2)}, u32[]{:S(2)}) collective-permute-start(bf16[64,2048]{1,0:T(8,128)(2,1)S(1)} %bitcast.321), channel_id=1, source_target_pairs={{0,4},{4,0},{8,12},{12,8},{16,20},{20,16},{24,28},{28,24},{1,5},{5... | collective-permute-start | bytes 786440 | tf_op jit(solution)/shard_map/ppermute | solution.py:178
  86.1 35.5 %collective-permute-start.34 = (bf16[64,2048]{1,0:T(8,128)(2,1)S(1)}, bf16[64,2048]{1,0:T(8,128)(2,1)S(1)}, u32[]{:S(2)}, u32[]{:S(2)}) collective-permute-start(bf16[64,2048]{1,0:T(8,128)(2,1)S(1)} %bitcast.323), channel_id=1, source_target_pairs={{0,4},{4,0},{8,12},{12,8},{16,20},{20,16},{24,28},{28,24},{1,5},{5... | collective-permute-start | bytes 786440 | tf_op jit(solution)/shard_map/ppermute | solution.py:178
  88.2 39.0 %collective-permute-start.24 = (bf16[64,2048]{1,0:T(8,128)(2,1)S(1)}, bf16[64,2048]{1,0:T(8,128)(2,1)S(1)}, u32[]{:S(2)}, u32[]{:S(2)}) collective-permute-start(bf16[64,2048]{1,0:T(8,128)(2,1)S(1)} %bitcast.325), channel_id=1, source_target_pairs={{0,4},{4,0},{8,12},{12,8},{16,20},{20,16},{24,28},{28,24},{1,5},{5... | collective-permute-start | bytes 786440 | tf_op jit(solution)/shard_map/ppermute | solution.py:178
  88.3 38.9 %collective-permute-start.23 = (bf16[64,2048]{1,0:T(8,128)(2,1)S(1)}, bf16[64,2048]{1,0:T(8,128)(2,1)S(1)}, u32[]{:S(2)}, u32[]{:S(2)}) collective-permute-start(bf16[64,2048]{1,0:T(8,128)(2,1)S(1)} %bitcast.327), channel_id=1, source_target_pairs={{0,4},{4,0},{8,12},{12,8},{16,20},{20,16},{24,28},{28,24},{1,5},{5... | collective-permute-start | bytes 786440 | tf_op jit(solution)/shard_map/ppermute | solution.py:178
  89.0 6.2 %collective-permute-start.9 = (bf16[2,16,2560]{2,1,0:T(8,128)(2,1)S(1)}, bf16[2,16,2560]{2,1,0:T(8,128)(2,1)S(1)}, u32[]{:S(2)}, u32[]{:S(2)}) collective-permute-start(bf16[2,16,2560]{2,1,0:T(8,128)(2,1)S(1)} %fusion.13), channel_id=1, source_target_pairs={{0,8},{4,12},{8,0},{12,4},{16,24},{20,28},{24,16},{28,20},{1,9},{5... | collective-permute-start | bytes 491528 | tf_op jit(solution)/shard_map/ppermute | solution.py:178
  95.1 5.3 %collective-permute-start.5 = (bf16[2,16,2560]{2,1,0:T(8,128)(2,1)S(1)}, bf16[2,16,2560]{2,1,0:T(8,128)(2,1)S(1)}, u32[]{:S(2)}, u32[]{:S(2)}) collective-permute-start(bf16[2,16,2560]{2,1,0:T(8,128)(2,1)S(1)} %fusion.12), channel_id=1, source_target_pairs={{0,16},{4,20},{8,24},{12,28},{16,0},{20,4},{24,8},{28,12},{1,17},{... | collective-permute-start | bytes 491528 | tf_op jit(solution)/shard_map/ppermute | solution.py:178
  110.2 5.3 %collective-permute-start.11 = (bf16[32,2560]{1,0:T(8,128)(2,1)S(1)}, bf16[32,2560]{1,0:T(8,128)(2,1)S(1)}, u32[]{:S(2)}, u32[]{:S(2)}) collective-permute-start(bf16[32,2560]{1,0:T(8,128)(2,1)S(1)} %bitcast.353), channel_id=1, source_target_pairs={{0,16},{4,20},{8,24},{12,28},{16,0},{20,4},{24,8},{28,12},{1,17},{... | collective-permute-start | bytes 491528 | tf_op jit(solution)/shard_map/ppermute | solution.py:178
  120.9 12.1 %collective-permute-start.13 = (bf16[64,2560]{1,0:T(8,128)(2,1)S(1)}, bf16[64,2560]{1,0:T(8,128)(2,1)S(1)}, u32[]{:S(2)}, u32[]{:S(2)}) collective-permute-start(bf16[64,2560]{1,0:T(8,128)(2,1)S(1)} %bitcast.317), channel_id=1, source_target_pairs={{0,4},{4,0},{8,12},{12,8},{16,20},{20,16},{24,28},{28,24},{1,5},{5... | collective-permute-start | bytes 983048 | tf_op jit(solution)/shard_map/ppermute | solution.py:178
  120.9 12.1 %collective-permute-start.12 = (bf16[64,2560]{1,0:T(8,128)(2,1)S(1)}, bf16[64,2560]{1,0:T(8,128)(2,1)S(1)}, u32[]{:S(2)}, u32[]{:S(2)}) collective-permute-start(bf16[64,2560]{1,0:T(8,128)(2,1)S(1)} %bitcast.319), channel_id=1, source_target_pairs={{0,4},{4,0},{8,12},{12,8},{16,20},{20,16},{24,28},{28,24},{1,5},{5... | collective-permute-start | bytes 983048 | tf_op jit(solution)/shard_map/ppermute | solution.py:178
  139.5 13.9 %collective-permute-start.36 = (bf16[64,2048]{1,0:T(8,128)(2,1)S(1)}, bf16[64,2048]{1,0:T(8,128)(2,1)S(1)}, u32[]{:S(2)}, u32[]{:S(2)}) collective-permute-start(bf16[64,2048]{1,0:T(8,128)(2,1)S(1)} %get-tuple-element.30), channel_id=1, source_target_pairs={{0,3},{1,0},{2,1},{3,2},{4,7},{5,4},{6,5},{7,6},{8,11},{9,8},{10,9... | collective-permute-start | bytes 786440 | tf_op jit(solution)/shard_map/ppermute | solution.py:181
  146.7 23.5 %collective-permute-start.37 = (bf16[64,2048]{1,0:T(8,128)(2,1)S(1)}, bf16[64,2048]{1,0:T(8,128)(2,1)S(1)}, u32[]{:S(2)}, u32[]{:S(2)}) collective-permute-start(bf16[64,2048]{1,0:T(8,128)(2,1)S(1)} %get-tuple-element.31), channel_id=1, source_target_pairs={{0,2},{1,3},{2,0},{3,1},{4,6},{5,7},{6,4},{7,5},{8,10},{9,11},{10,... | collective-permute-start | bytes 786440 | tf_op jit(solution)/shard_map/ppermute | solution.py:181
  147.1 23.1 %collective-permute-start.38 = (bf16[64,2048]{1,0:T(8,128)(2,1)S(1)}, bf16[64,2048]{1,0:T(8,128)(2,1)S(1)}, u32[]{:S(2)}, u32[]{:S(2)}) collective-permute-start(bf16[64,2048]{1,0:T(8,128)(2,1)S(1)} %get-tuple-element.32), channel_id=1, source_target_pairs={{0,1},{1,2},{2,3},{3,0},{4,5},{5,6},{6,7},{7,4},{8,9},{9,10},{10,1... | collective-permute-start | bytes 786440 | tf_op jit(solution)/shard_map/ppermute | solution.py:181
  (8 other events, 51.0 us)

commit v2 on v1

--- a/solution.py
+++ b/solution.py
@@ -7,7 +7,8 @@
 
 F32 = jnp.float32
 BF16 = jnp.bfloat16
-PIECES = (4, 4, 5)
+PIECES = (4, 5, 4)
+GROUPS = (((0, 1, 2),), ((0,), (1, 2)))
 HELD = ((0, 0), (0, 1), (1, 0), (1, 1))
 
 
@@ -103,7 +104,7 @@
             tile = w[:, cols] if held[i] else w[...]
             part = jnp.dot(x[...], tile, preferred_element_type=F32)
             keep[i] = part[:half]
-            send[i] = part[half:].astype(BF16)
+            send[i] = part[half:].astype(send.dtype)
 
     o_spec = pl.BlockSpec((2, half, bn), lambda j: (0, 0, j))
     stream = pl.BlockSpec((k, bn), lambda j: (0, first + j))
@@ -115,60 +116,86 @@
         out_specs=[o_spec, o_spec],
         out_shape=[
             jax.ShapeDtypeStruct((2, half, n * bn), F32),
-            jax.ShapeDtypeStruct((2, half, n * bn), BF16),
+            jax.ShapeDtypeStruct((2, half, n * bn), F32),
         ],
-        compiler_params=params(5 if all(held) else 45),
+        compiler_params=params(5 if all(held) else 39),
         cost_estimate=cost(rows, k, 2 * n * bn),
     )(feats, *pair)
 
 
-def down(me, hiddens, acc, down_weight, start, groups, owners):
-    w = hiddens[0].shape[1]
-    rows, n = sum(h.shape[0] for h in hiddens), down_weight.shape[1]
-    step = rows // (2 * groups)
+def fetch_rows(weight, chunks, bn):
+    n = weight.shape[1]
+    shapes = [pltpu.VMEM(((last - first) * bn, n), BF16) for first, last in chunks]
+    count = len(chunks)
+
+    def kernel(w, *refs):
+        outs, sems = refs[:-1], refs[-1]
+        copies = []
+        for i, (first, last) in enumerate(chunks):
+            rows = pl.ds(first * bn, (last - first) * bn)
+            copies.append(pltpu.make_async_copy(w.at[rows], outs[i], sems.at[i]))
+        for c in copies:
+            c.start()
+        for c in copies:
+            c.wait()
+
+    return pl.pallas_call(
+        kernel,
+        in_specs=[pl.BlockSpec(memory_space=pl.ANY)],
+        out_specs=[pl.BlockSpec(memory_space=pltpu.VMEM)] * count,
+        out_shape=shapes,
+        scratch_shapes=[pltpu.SemaphoreType.DMA((count,))],
+        compiler_params=params(14),
+        cost_estimate=pl.CostEstimate(flops=0, transcendentals=0, bytes_accessed=4 * weight.size),
+    )(weight)
+
+
+def down(me, mine, other, acc, held, groups, kinds):
+    w = mine.shape[1]
+    rows, n = 2 * mine.shape[0], held[0].shape[1]
+    step = rows // groups
     bn = block_of(n)
-    count = len(hiddens)
+    count = len(held)
 
     def kernel(me_ref, *refs):
-        refs = list(refs)
-        ins, wd = refs[:count], refs[count]
-        prev = refs[count + 1] if acc is not None else None
-        outs, lhs = refs[count + 1 + (acc is not None) : -1], refs[-1]
+        a, b, wds = refs[0], refs[1], refs[2 : 2 + count]
+        outs, lhs = refs[2 + count + (acc is not None) : -1], refs[-1]
 
         @pl.when(pl.program_id(0) == 0)
         def _():
-            per = len(row_blocks(groups)) // count
-            for i, (h, p) in enumerate(row_blocks(groups)):
-                at = (i % per) * step
-                dst = pl.multiple_of((h * groups + (me_ref[0] ^ p)) * step, step)
-                lhs[pl.ds(dst, step), :] = ins[i // per][at : at + step, :]
-
-        total = jnp.dot(lhs[...], wd[...], preferred_element_type=F32)
-        if prev is not None:
-            total = total + prev[...]
+            for p in range(groups):
+                dst = pl.multiple_of((me_ref[0] ^ p) * step, step)
+                lhs[pl.ds(dst, step), :] = (a, b)[p % 2][p // 2 * step : (p // 2 + 1) * step, :]
+
+        cols = pl.ds(pl.multiple_of(pl.program_id(0) * bn, bn), bn)
+        total = None if acc is None else refs[2 + count][...]
+        at = 0
+        for wd in wds:
+            part = jnp.dot(lhs[:, at : at + wd.shape[0]], wd[:, cols], preferred_element_type=F32)
+            total = part if total is None else total + part
+            at += wd.shape[0]
         each = rows // len(outs)
         for s, o in enumerate(outs):
             o[...] = total[s * each : (s + 1) * each].astype(o.dtype)
 
-    in_specs = [pl.BlockSpec(h.shape, lambda j, m: (0, 0)) for h in hiddens]
-    in_specs.append(pl.BlockSpec((pl.Element(w), pl.Element(bn)), lambda j, m: (start, j * bn)))
-    args = [*hiddens, down_weight]
+    h_spec = pl.BlockSpec(mine.shape, lambda j, m: (0, 0))
+    in_specs = [h_spec, h_spec] + [pl.BlockSpec(memory_space=pltpu.VMEM)] * count
+    args = [mine, other, *held]
     if acc is not None:
         in_specs.append(pl.BlockSpec((rows, bn), lambda j, m: (0, j)))
         args.append(acc)
-    each = rows // owners
-    out_shape = [jax.ShapeDtypeStruct((each, n), F32 if s == 0 else BF16) for s in range(owners)]
+    each = rows // len(kinds)
     return pl.pallas_call(
         kernel,
         grid_spec=pltpu.PrefetchScalarGridSpec(
             num_scalar_prefetch=1,
             grid=(n // bn,),
             in_specs=in_specs,
-            out_specs=[pl.BlockSpec((each, bn), lambda j, m: (0, j))] * owners,
+            out_specs=[pl.BlockSpec((each, bn), lambda j, m: (0, j))] * len(kinds),
             scratch_shapes=[pltpu.VMEM((rows, w), BF16)],
         ),
-        out_shape=out_shape,
-        compiler_params=params(40),
+        out_shape=[jax.ShapeDtypeStruct((each, n), k) for k in kinds],
+        compiler_params=params(12),
         cost_estimate=cost(rows, w, n),
     )(me, *args)
 
@@ -177,15 +204,15 @@
     def swap(v, mask):
         return lax.ppermute(v, "gx", [(i, i ^ mask) for i in range(nx)])
 
-    def shift(v, s):
-        return lax.ppermute(v, "gy", [(i, (i + s) % nz) for i in range(nz)])
+    def across(v, mask):
+        return lax.ppermute(v, "gy", [(i, i ^ mask) for i in range(nz)])
 
     chips = nx // 2
     bits = chips.bit_length() - 1
 
     def layer(tokens, gate_weight, up_weight, down_weight):
         me = lax.axis_index("gx").astype(jnp.int32).reshape(1)
-        parts = [tokens] + [shift(tokens, s) for s in range(1, nz)]
+        parts = [tokens] + [across(tokens, s) for s in range(1, nz)]
         feats = place_rows(me, parts, nx)
         hid = gate_weight.shape[1]
         bn = block_of(hid)
@@ -197,36 +224,42 @@
         for (c, i), v in zip(HELD, got):
             weights[c][i] = v
         own = feats.shape[0] // (2 * nx)
-        acc = None
+        hiddens = {}
         for c, (first, last) in enumerate(chunks):
             keep, send = gate_up(feats, weights[c], [(c, i) in HELD for i in range(2)], first, last, bn)
             got = swap(send, 1)
-            halves = []
             for h in range(2):
-                order = range(bits) if h == 0 else range(bits)[::-1]
+                order = range(bits) if (h + c) % 2 else range(bits)[::-1]
                 rows = slice(h * chips * own, (h + 1) * chips * own)
-                block = keep[:, rows] + got[:, rows].astype(F32)
+                block = keep[:, rows] + got[:, rows]
                 for i, b in enumerate(order):
-                    wide = block.reshape(2, -1, 2, block.shape[1] // 2 ** (1 + sum(1 for o in order[i + 1 :] if o > b)), block.shape[2])
+                    inner = own * 2 ** sum(1 for o in order[i + 1 :] if o < b)
+                    wide = block.reshape(2, -1, 2, inner, block.shape[2])
                     stay, go = wide[:, :, 0], wide[:, :, 1].astype(BF16)
                     flat = (2, block.shape[1] // 2, block.shape[2])
                     come = swap(go.reshape(flat), 2 << b)
                     block = stay.reshape(flat) + come.astype(F32)
-                hidden = (jax.nn.silu(block[0]) * block[1]).astype(BF16)
-                for i, b in reversed(list(enumerate(order))):
-                    come = swap(hidden, 2 << b)
-                    inner = own * 2 ** sum(1 for o in order[i + 1 :] if o < b)
-                    both = [v.reshape(-1, 1, inner, v.shape[1]) for v in (hidden, come)]
-                    hidden = jnp.concatenate(both, axis=1).reshape(-1, hidden.shape[1])
-                halves.append(hidden)
-            halves += [swap(v, 1) for v in halves]
-            final = c == len(chunks) - 1
-            acc = down(me, halves, acc, down_weight, first * bn, nx, nz if final else 1)
-            acc = acc if final else acc[0]
-        out = acc[0]
-        for s in range(1, nz):
-            out = out + shift(acc[s], -s).astype(F32)
-        return out.astype(BF16)
+                hiddens[h, c] = (jax.nn.silu(block[0]) * block[1]).astype(BF16)
+        held = fetch_rows(down_weight, chunks, bn)
+        outs = {}
+        for h in (1, 0):
+            acc = None
+            for g, group in enumerate(GROUPS[h]):
+                hidden = jnp.concatenate([hiddens[h, c] for c in group], axis=1)
+                every = [hidden] + [swap(hidden, 2 * q) for q in range(1, chips)]
+                mine = jnp.concatenate(every, axis=0)
+                other = swap(mine, 1)
+                last = g == len(GROUPS[h]) - 1
+                kinds = [F32] if not last else [BF16 if h or s else F32 for s in range(nz // 2)]
+                acc = down(me, mine, other, acc, [held[c] for c in group], nx, kinds)
+                acc = acc if last else acc[0]
+            for s in range(nz // 2):
+                outs[h * nz // 2 + s] = acc[s]
+        total = outs[0]
+        for s in list(range(nz // 2, nz)) + list(range(1, nz // 2)):
+            come = across(outs[s], s)
+            total = total + come.astype(F32)
+        return total.astype(BF16)
 
     return layer
 

time: 171 us -> 165 us (0.965)
  starting transfers between devices: 43.9 us -> 37.9 us
  waiting for transfers between devices: 73 us -> 68.3 us
  Pallas kernels: 50 us -> 53 us
    ppermute x33 -> x27, waiting for transfers between devices: 44.8 us -> 33.3 us  [swap(): return lax.ppermute(v, 'gx', [(i, i ^ mask) for i in range(nx)])]
    pallas_call x0 -> x1, Pallas kernels: none -> 8.78 us  [fetch_rows(): pl.pallas_call(kernel, in_specs=[pl.BlockSpec(memory_space=pl.ANY)], out_...]
    pallas_call x3, Pallas kernels: 18 us -> 10.5 us  [down(): pl.pallas_call(kernel, grid_spec=pltpu.PrefetchScalarGridSpec(num_scalar_...]
    ppermute x6, waiting for transfers between devices: 28.2 us -> 35 us  [across(): return lax.ppermute(v, 'gy', [(i, i ^ mask) for i in range(nz)])]
    ppermute x33 -> x27, starting transfers between devices: 29.1 us -> 25.8 us  [swap(): return lax.ppermute(v, 'gx', [(i, i ^ mask) for i in range(nx)])]
    ppermute x6, starting transfers between devices: 14.8 us -> 12.1 us  [across(): return lax.ppermute(v, 'gy', [(i, i ^ mask) for i in range(nz)])]
  transfers between devices with their start and end apart: 39 -> 33, of which waited for: 18 -> 17; matrix products, arithmetic and copies ran while one was open for 2% -> 2% of each run, Pallas kernels for 22% -> 26%
where the time goes in v2:
time: 165 us
  waiting for transfers between devices  68.3 us (41%)
  Pallas kernels  53 us (32%)
  starting transfers between devices  37.9 us (23%)
  other arithmetic  4.22 us (3%)
    ppermute x6, waiting for transfers between devices, across(): return lax.ppermute(v, 'gy', [(i, i ^ mask) for i in range(nz)])  35 us
    ppermute x27, waiting for transfers between devices, swap(): return lax.ppermute(v, 'gx', [(i, i ^ mask) for i in range(nx)])  33.3 us
    ppermute x27, starting transfers between devices, swap(): return lax.ppermute(v, 'gx', [(i, i ^ mask) for i in range(nx)])  25.8 us
    pallas_call x3, Pallas kernels, gate_up(): pl.pallas_call(kernel, grid=(n,), in_specs=[pl.BlockSpec((rows, k), lambd...  21.6 us
    ppermute x6, starting transfers between devices, across(): return lax.ppermute(v, 'gy', [(i, i ^ mask) for i in range(nz)])  12.1 us
    pallas_call x1, Pallas kernels, fetch(): pl.pallas_call(kernel, in_specs=[pl.BlockSpec(memory_space=pl.ANY)] * len...  12 us
    pallas_call x3, Pallas kernels, down(): pl.pallas_call(kernel, grid_spec=pltpu.PrefetchScalarGridSpec(num_scalar_...  10.5 us
    pallas_call x1, Pallas kernels, fetch_rows(): pl.pallas_call(kernel, in_specs=[pl.BlockSpec(memory_space=pl.ANY)], out_...  8.78 us
  transfers between devices with their start and end apart: 33, of which 17 were waited for; matrix products, arithmetic and copies ran while one was open for 2% of the time, Pallas kernels for 26%

profile of v2, /device:TPU:0, one launch (start us, length us, event | category | flops | bytes accessed | tf_op | source)
XLA Modules:
  0.0 165.2 jit_solution(2082927867913115424)
XLA Ops:
  0.0 3.1 %collective-permute-start = (bf16[64,2048]{1,0:T(8,128)(2,1)}, bf16[64,2048]{1,0:T(8,128)(2,1)S(1)}, u32[]{:S(2)}, u32[]{:S(2)}) collective-permute-start(bf16[64,2048]{1,0:T(8,128)(2,1)} %refs_0_.2), channel_id=1, source_target_pairs={{0,1},{1,0},{2,3},{3,2},{4,5},{5,4},{6,7},{7,6},{8,9},{9,8},{10,11... | collective-permute-start | bytes 786440 | tf_op jit(solution)/shard_map/ppermute | solution.py:208
  3.1 2.6 %collective-permute-start.1 = (bf16[64,2048]{1,0:T(8,128)(2,1)}, bf16[64,2048]{1,0:T(8,128)(2,1)S(1)}, u32[]{:S(2)}, u32[]{:S(2)}) collective-permute-start(bf16[64,2048]{1,0:T(8,128)(2,1)} %refs_0_.2), channel_id=1, source_target_pairs={{0,2},{1,3},{2,0},{3,1},{4,6},{5,7},{6,4},{7,5},{8,10},{9,11},{10,... | collective-permute-start | bytes 786440 | tf_op jit(solution)/shard_map/ppermute | solution.py:208
  5.6 8.8 %collective-permute-done.refs_1_ = bf16[64,2048]{1,0:T(8,128)(2,1)S(1)} collective-permute-done((bf16[64,2048]{1,0:T(8,128)(2,1)}, bf16[64,2048]{1,0:T(8,128)(2,1)S(1)}, u32[]{:S(2)}, u32[]{:S(2)}) %collective-permute-start) | collective-permute-done | bytes 262176 | tf_op jit(solution)/shard_map/ppermute | solution.py:208
  14.4 10.1 %collective-permute-done.1.refs_2_ = bf16[64,2048]{1,0:T(8,128)(2,1)S(1)} collective-permute-done((bf16[64,2048]{1,0:T(8,128)(2,1)}, bf16[64,2048]{1,0:T(8,128)(2,1)S(1)}, u32[]{:S(2)}, u32[]{:S(2)}) %collective-permute-start.1) | collective-permute-done | bytes 262176 | tf_op jit(solution)/shard_map/ppermute | solution.py:208
  25.7 9.7 %shard_map.50 = (f32[2,128,2048]{2,1,0:T(8,128)S(1)}, f32[2,128,2048]{2,1,0:T(8,128)}) custom-call(bf16[256,2048]{1,0:T(8,128)(2,1)S(1)} %shard_map.46.x, bf16[2048,6656]{1,0:T(8,128)(2,1)} %g.1, bf16[2048,6656]{1,0:T(8,128)(2,1)} %u.1), custom_call_target="tpu_custom_call" | custom-call | flops 4294967296 | bytes 22020096 | tf_op jit(solution)/shard_map/pallas_call | solution.py:111
  35.4 12.0 %shard_map.47 = (bf16[2048,2048]{1,0:T(8,128)(2,1)S(1)}, bf16[2048,2048]{1,0:T(8,128)(2,1)S(1)}, bf16[2048,2560]{1,0:T(8,128)(2,1)S(1)}, bf16[2048,2560]{1,0:T(8,128)(2,1)S(1)}) custom-call(bf16[2048,6656]{1,0:T(8,128)(2,1)} %g.1, bf16[2048,6656]{1,0:T(8,128)(2,1)} %u.1), custom_call_target="tpu_custom_call" | custom-call | bytes 54525952 | tf_op jit(solution)/shard_map/pallas_call | solution.py:86
  47.4 5.3 %shard_map.48 = (f32[2,128,2048]{2,1,0:T(8,128)S(1)}, f32[2,128,2048]{2,1,0:T(8,128)S(1)}) custom-call(bf16[256,2048]{1,0:T(8,128)(2,1)S(1)} %shard_map.46.x, bf16[2048,2048]{1,0:T(8,128)(2,1)S(1)} %get-tuple-element.22.g, bf16[2048,2048]{1,0:T(8,128)(2,1)S(1)} %get-tuple-element.23.u), custom_call_target="tpu_custom_call" | custom-call | flops 4294967296 | bytes 22020096 | tf_op jit(solution)/shard_map/pallas_call | solution.py:111
  53.3 6.5 %shard_map.49 = (f32[2,128,2560]{2,1,0:T(8,128)S(1)}, f32[2,128,2560]{2,1,0:T(8,128)S(1)}) custom-call(bf16[256,2048]{1,0:T(8,128)(2,1)S(1)} %shard_map.46.x, bf16[2048,2560]{1,0:T(8,128)(2,1)S(1)} %get-tuple-element.26.g, bf16[2048,2560]{1,0:T(8,128)(2,1)S(1)} %get-tuple-element.27.u), custom_call_target="tpu_custom_call" | custom-call | flops 5368709120 | bytes 27262976 | tf_op jit(solution)/shard_map/pallas_call | solution.py:111
  60.3 1.8 %slice_add_fusion.2 = (f32[2,64,2048]{2,1,0:T(8,128)S(1)}, f32[2,64,2048]{2,1,0:T(8,128)S(1)}) fusion(f32[2,128,2048]{2,1,0:T(8,128)} %collective-permute-done.3, f32[2,128,2048]{2,1,0:T(8,128)S(1)} %get-tuple-element.24), kind=kLoop, calls=%fused_computation.2 | loop fusion | flops 524288 | bytes 6291456 | tf_op jit(solution)/shard_map/add | solution.py:234
  62.3 1.6 collective-permute-start.10
  66.5 5.0 %collective-permute-done.10 = bf16[2,32,2048]{2,1,0:T(8,128)(2,1)S(1)} collective-permute-done((bf16[2,32,2048]{2,1,0:T(8,128)(2,1)S(1)}, bf16[2,32,2048]{2,1,0:T(8,128)(2,1)S(1)}, u32[]{:S(2)}, u32[]{:S(2)}) %collective-permute-start.10) | collective-permute-done | bytes 262176 | tf_op jit(solution)/shard_map/ppermute | solution.py:205
  71.6 1.6 collective-permute-start.11
  73.2 3.5 %collective-permute-done.4 = bf16[2,32,2048]{2,1,0:T(8,128)(2,1)S(1)} collective-permute-done((bf16[2,32,2048]{2,1,0:T(8,128)(2,1)S(1)}, bf16[2,32,2048]{2,1,0:T(8,128)(2,1)S(1)}, u32[]{:S(2)}, u32[]{:S(2)}) %collective-permute-start.4) | collective-permute-done | bytes 262176 | tf_op jit(solution)/shard_map/ppermute | solution.py:205
  76.7 1.6 collective-permute-start.5
  79.3 1.6 collective-permute-start.25
  81.6 3.0 %collective-permute-done.25 = bf16[2,16,2048]{2,1,0:T(8,128)(2,1)S(1)} collective-permute-done((bf16[2,16,2048]{2,1,0:T(8,128)(2,1)S(1)}, bf16[2,16,2048]{2,1,0:T(8,128)(2,1)S(1)}, u32[]{:S(2)}, u32[]{:S(2)}) %collective-permute-start.25) | collective-permute-done | bytes 131104 | tf_op jit(solution)/shard_map/ppermute | solution.py:205
  84.7 2.3 %collective-permute-start.28 = (bf16[16,2048]{1,0:T(8,128)(2,1)S(1)}, bf16[16,2048]{1,0:T(8,128)(2,1)S(1)}, u32[]{:S(2)}, u32[]{:S(2)}) collective-permute-start(bf16[16,2048]{1,0:T(8,128)(2,1)S(1)} %fusion.23), channel_id=1, source_target_pairs={{0,24},{4,28},{8,16},{12,20},{16,8},{20,12},{24,0},{28,4},{1,25},{... | collective-permute-start | bytes 196616 | tf_op jit(solution)/shard_map/ppermute | solution.py:205
  90.9 4.4 %collective-permute-done.7 = bf16[2,32,2560]{2,1,0:T(8,128)(2,1)S(1)} collective-permute-done((bf16[2,32,2560]{2,1,0:T(8,128)(2,1)S(1)}, bf16[2,32,2560]{2,1,0:T(8,128)(2,1)S(1)}, u32[]{:S(2)}, u32[]{:S(2)}) %collective-permute-start.7) | collective-permute-done | bytes 327712 | tf_op jit(solution)/shard_map/ppermute | solution.py:205
  95.4 1.6 collective-permute-start.8
  96.9 1.5 collective-permute-done.16
  100.9 2.0 %collective-permute-start.14 = (bf16[16,6656]{1,0:T(8,128)(2,1)S(1)}, bf16[16,6656]{1,0:T(8,128)(2,1)S(1)}, u32[]{:S(2)}, u32[]{:S(2)}) collective-permute-start(bf16[16,6656]{1,0:T(8,128)(2,1)S(1)} %pad_maximum_fusion.3), channel_id=1, source_target_pairs={{0,24},{4,28},{8,16},{12,20},{16,8},{20,12},{24,0},{28,4},{1,25},{... | collective-permute-start | bytes 638984 | tf_op jit(solution)/shard_map/ppermute | solution.py:205
  103.7 2.0 %collective-permute-done.17 = bf16[2,16,2560]{2,1,0:T(8,128)(2,1)S(1)} collective-permute-done((bf16[2,16,2560]{2,1,0:T(8,128)(2,1)S(1)}, bf16[2,16,2560]{2,1,0:T(8,128)(2,1)S(1)}, u32[]{:S(2)}, u32[]{:S(2)}) %collective-permute-start.17) | collective-permute-done | bytes 163872 | tf_op jit(solution)/shard_map/ppermute | solution.py:205
  106.8 4.4 %collective-permute-done.14 = bf16[16,6656]{1,0:T(8,128)(2,1)S(1)} collective-permute-done((bf16[16,6656]{1,0:T(8,128)(2,1)S(1)}, bf16[16,6656]{1,0:T(8,128)(2,1)S(1)}, u32[]{:S(2)}, u32[]{:S(2)}) %collective-permute-start.14) | collective-permute-done | bytes 213024 | tf_op jit(solution)/shard_map/ppermute | solution.py:205
  115.9 2.2 %collective-permute-done.22 = bf16[16,4608]{1,0:T(8,128)(2,1)S(1)} collective-permute-done((bf16[16,4608]{1,0:T(8,128)(2,1)S(1)}, bf16[16,4608]{1,0:T(8,128)(2,1)S(1)}, u32[]{:S(2)}, u32[]{:S(2)}) %collective-permute-start.22) | collective-permute-done | bytes 147488 | tf_op jit(solution)/shard_map/ppermute | solution.py:205
  120.1 2.2 %collective-permute-done.26 = bf16[16,2048]{1,0:T(8,128)(2,1)S(1)} collective-permute-done((bf16[16,2048]{1,0:T(8,128)(2,1)S(1)}, bf16[16,2048]{1,0:T(8,128)(2,1)S(1)}, u32[]{:S(2)}, u32[]{:S(2)}) %collective-permute-start.26) | collective-permute-done | bytes 65568 | tf_op jit(solution)/shard_map/ppermute | solution.py:205
  122.4 8.8 %shard_map.51 = (bf16[2048,2048]{1,0:T(8,128)(2,1)S(1)}, bf16[2560,2048]{1,0:T(8,128)(2,1)S(1)}, bf16[2048,2048]{1,0:T(8,128)(2,1)S(1)}) custom-call(bf16[6656,2048]{1,0:T(8,128)(2,1)} %w.1), custom_call_target="tpu_custom_call" | custom-call | bytes 54525952 | tf_op jit(solution)/shard_map/pallas_call | solution.py:142
  131.2 2.0 %shard_map.53.refs_4_ = f32[128,2048]{1,0:T(8,128)S(1)} custom-call(s32[1]{0:T(128)} %bitcast.me_ref, bf16[64,2048]{1,0:T(8,128)(2,1)S(1)} %pad_maximum_fusion.2.refs_0_, bf16[64,2048]{1,0:T(8,128)(2,1)S(1)} %collective-permute-done.29.refs_1_, bf16[2048,2048]{1,0:T(8,128)(2,1)S(1)} %get-tuple-element.32.refs_2_), custom_call_target="tpu_custom_call" | custom-call | flops 1073741824 | bytes 9961472 | tf_op jit(solution)/shard_map/pallas_call | solution.py:188
  133.3 3.7 %shard_map.54 = (bf16[64,2048]{1,0:T(8,128)(2,1)S(1)}, bf16[64,2048]{1,0:T(8,128)(2,1)S(1)}) custom-call(s32[1]{0:T(128)} %bitcast.me_ref, bf16[64,4608]{1,0:T(8,128)(2,1)S(1)} %pad_maximum_fusion.1.refs_0_, bf16[64,4608]{1,0:T(8,128)(2,1)S(1)} %collective-permute-done.23.refs_1_, bf16[2560,2048]{1,0:T(8,128)(2,1)S(1)} %get-tuple-element.33.refs_3_.refs_2_, ...), custom_call_target="tpu_custom_call" | custom-call | flops 2415919104 | bytes 21102592 | tf_op jit(solution)/shard_map/pallas_call | solution.py:188
  137.0 2.5 %collective-permute-start.31 = (bf16[64,2048]{1,0:T(8,128)(2,1)S(1)}, bf16[64,2048]{1,0:T(8,128)(2,1)S(1)}, u32[]{:S(2)}, u32[]{:S(2)}) collective-permute-start(bf16[64,2048]{1,0:T(8,128)(2,1)S(1)} %get-tuple-element.37), channel_id=1, source_target_pairs={{0,3},{1,2},{2,1},{3,0},{4,7},{5,6},{6,5},{7,4},{8,11},{9,10},{10,... | collective-permute-start | bytes 786440 | tf_op jit(solution)/shard_map/ppermute | solution.py:208
  139.5 3.8 %collective-permute-start.30 = (bf16[64,2048]{1,0:T(8,128)(2,1)S(1)}, bf16[64,2048]{1,0:T(8,128)(2,1)S(1)}, u32[]{:S(2)}, u32[]{:S(2)}) collective-permute-start(bf16[64,2048]{1,0:T(8,128)(2,1)S(1)} %get-tuple-element.36), channel_id=1, source_target_pairs={{0,2},{1,3},{2,0},{3,1},{4,6},{5,7},{6,4},{7,5},{8,10},{9,11},{10,... | collective-permute-start | bytes 786440 | tf_op jit(solution)/shard_map/ppermute | solution.py:208
  143.3 4.8 %shard_map.52 = (f32[64,2048]{1,0:T(8,128)S(1)}, bf16[64,2048]{1,0:T(8,128)(2,1)S(1)}) custom-call(s32[1]{0:T(128)} %bitcast.me_ref, bf16[64,6656]{1,0:T(8,128)(2,1)S(1)} %pad_maximum_fusion.refs_0_, bf16[64,6656]{1,0:T(8,128)(2,1)S(1)} %collective-permute-done.15.refs_1_, bf16[2048,2048]{1,0:T(8,128)(2,1)S(1)} %get-tuple-element.32.refs_2_, ...), custom_call_target="tpu_custom_call" | custom-call | flops 3489660928 | bytes 30015488 | tf_op jit(solution)/shard_map/pallas_call | solution.py:188
  148.3 16.1 %collective-permute-done.30 = bf16[64,2048]{1,0:T(8,128)(2,1)S(1)} collective-permute-done((bf16[64,2048]{1,0:T(8,128)(2,1)S(1)}, bf16[64,2048]{1,0:T(8,128)(2,1)S(1)}, u32[]{:S(2)}, u32[]{:S(2)}) %collective-permute-start.30) | collective-permute-done | bytes 262176 | tf_op jit(solution)/shard_map/ppermute | solution.py:208
  (87 shorter events, 22.7 us)
Async XLA Ops:
  0.0 14.4 %collective-permute-start = (bf16[64,2048]{1,0:T(8,128)(2,1)}, bf16[64,2048]{1,0:T(8,128)(2,1)S(1)}, u32[]{:S(2)}, u32[]{:S(2)}) collective-permute-start(bf16[64,2048]{1,0:T(8,128)(2,1)} %refs_0_.2), channel_id=1, source_target_pairs={{0,1},{1,0},{2,3},{3,2},{4,5},{5,4},{6,7},{7,6},{8,9},{9,8},{10,11... | collective-permute-start | bytes 786440 | tf_op jit(solution)/shard_map/ppermute | solution.py:208
  3.1 21.5 %collective-permute-start.1 = (bf16[64,2048]{1,0:T(8,128)(2,1)}, bf16[64,2048]{1,0:T(8,128)(2,1)S(1)}, u32[]{:S(2)}, u32[]{:S(2)}) collective-permute-start(bf16[64,2048]{1,0:T(8,128)(2,1)} %refs_0_.2), channel_id=1, source_target_pairs={{0,2},{1,3},{2,0},{3,1},{4,6},{5,7},{6,4},{7,5},{8,10},{9,11},{10,... | collective-permute-start | bytes 786440 | tf_op jit(solution)/shard_map/ppermute | solution.py:208
  5.6 18.9 %collective-permute-start.2 = (bf16[64,2048]{1,0:T(8,128)(2,1)}, bf16[64,2048]{1,0:T(8,128)(2,1)S(1)}, u32[]{:S(2)}, u32[]{:S(2)}) collective-permute-start(bf16[64,2048]{1,0:T(8,128)(2,1)} %refs_0_.2), channel_id=1, source_target_pairs={{0,3},{1,2},{2,1},{3,0},{4,7},{5,6},{6,5},{7,4},{8,11},{9,10},{10,... | collective-permute-start | bytes 786440 | tf_op jit(solution)/shard_map/ppermute | solution.py:208
  35.4 24.5 %collective-permute-start.9 = (f32[2,128,2048]{2,1,0:T(8,128)}, f32[2,128,2048]{2,1,0:T(8,128)S(1)}, u32[]{:S(2)}, u32[]{:S(2)}) collective-permute-start(f32[2,128,2048]{2,1,0:T(8,128)} %get-tuple-element.31), channel_id=1, source_target_pairs={{0,4},{4,0},{8,12},{12,8},{16,20},{20,16},{24,28},{28,24},{1,5},{5... | collective-permute-start | bytes 6291464 | tf_op jit(solution)/shard_map/ppermute | solution.py:205
  52.7 7.6 %collective-permute-start.3 = (f32[2,128,2048]{2,1,0:T(8,128)S(1)}, f32[2,128,2048]{2,1,0:T(8,128)}, u32[]{:S(2)}, u32[]{:S(2)}) collective-permute-start(f32[2,128,2048]{2,1,0:T(8,128)S(1)} %get-tuple-element.25), channel_id=1, source_target_pairs={{0,4},{4,0},{8,12},{12,8},{16,20},{20,16},{24,28},{28,24},{1,5},{5... | collective-permute-start | bytes 6291464 | tf_op jit(solution)/shard_map/ppermute | solution.py:205
  59.8 27.9 %collective-permute-start.6 = (f32[2,128,2560]{2,1,0:T(8,128)S(1)}, f32[2,128,2560]{2,1,0:T(8,128)S(1)}, u32[]{:S(2)}, u32[]{:S(2)}) collective-permute-start(f32[2,128,2560]{2,1,0:T(8,128)S(1)} %get-tuple-element.29), channel_id=1, source_target_pairs={{0,4},{4,0},{8,12},{12,8},{16,20},{20,16},{24,28},{28,24},{1,5},{5... | collective-permute-start | bytes 7864328 | tf_op jit(solution)/shard_map/ppermute | solution.py:205
  62.3 9.2 %collective-permute-start.10 = (bf16[2,32,2048]{2,1,0:T(8,128)(2,1)S(1)}, bf16[2,32,2048]{2,1,0:T(8,128)(2,1)S(1)}, u32[]{:S(2)}, u32[]{:S(2)}) collective-permute-start(bf16[2,32,2048]{2,1,0:T(8,128)(2,1)S(1)} %fusion.7), channel_id=1, source_target_pairs={{0,16},{4,20},{8,24},{12,28},{16,0},{20,4},{24,8},{28,12},{1,17},{... | collective-permute-start | bytes 786440 | tf_op jit(solution)/shard_map/ppermute | solution.py:205
  63.9 12.7 %collective-permute-start.4 = (bf16[2,32,2048]{2,1,0:T(8,128)(2,1)S(1)}, bf16[2,32,2048]{2,1,0:T(8,128)(2,1)S(1)}, u32[]{:S(2)}, u32[]{:S(2)}) collective-permute-start(bf16[2,32,2048]{2,1,0:T(8,128)(2,1)S(1)} %fusion.6), channel_id=1, source_target_pairs={{0,16},{4,20},{8,24},{12,28},{16,0},{20,4},{24,8},{28,12},{1,17},{... | collective-permute-start | bytes 786440 | tf_op jit(solution)/shard_map/ppermute | solution.py:205
  64.5 16.5 %collective-permute-start.18 = (bf16[2,32,2048]{2,1,0:T(8,128)(2,1)S(1)}, bf16[2,32,2048]{2,1,0:T(8,128)(2,1)S(1)}, u32[]{:S(2)}, u32[]{:S(2)}) collective-permute-start(bf16[2,32,2048]{2,1,0:T(8,128)(2,1)S(1)} %bitcast.161), channel_id=1, source_target_pairs={{0,8},{4,12},{8,0},{12,4},{16,24},{20,28},{24,16},{28,20},{1,9},{5... | collective-permute-start | bytes 786440 | tf_op jit(solution)/shard_map/ppermute | solution.py:205
  66.0 13.3 %collective-permute-start.24 = (bf16[2,32,2048]{2,1,0:T(8,128)(2,1)S(1)}, bf16[2,32,2048]{2,1,0:T(8,128)(2,1)S(1)}, u32[]{:S(2)}, u32[]{:S(2)}) collective-permute-start(bf16[2,32,2048]{2,1,0:T(8,128)(2,1)S(1)} %bitcast.162), channel_id=1, source_target_pairs={{0,8},{4,12},{8,0},{12,4},{16,24},{20,28},{24,16},{28,20},{1,9},{5... | collective-permute-start | bytes 786440 | tf_op jit(solution)/shard_map/ppermute | solution.py:205
  71.6 15.4 %collective-permute-start.11 = (bf16[2,16,2048]{2,1,0:T(8,128)(2,1)S(1)}, bf16[2,16,2048]{2,1,0:T(8,128)(2,1)S(1)}, u32[]{:S(2)}, u32[]{:S(2)}) collective-permute-start(bf16[2,16,2048]{2,1,0:T(8,128)(2,1)S(1)} %fusion.19), channel_id=1, source_target_pairs={{0,8},{4,12},{8,0},{12,4},{16,24},{20,28},{24,16},{28,20},{1,9},{5... | collective-permute-start | bytes 393224 | tf_op jit(solution)/shard_map/ppermute | solution.py:205
  76.7 10.8 %collective-permute-start.5 = (bf16[2,16,2048]{2,1,0:T(8,128)(2,1)S(1)}, bf16[2,16,2048]{2,1,0:T(8,128)(2,1)S(1)}, u32[]{:S(2)}, u32[]{:S(2)}) collective-permute-start(bf16[2,16,2048]{2,1,0:T(8,128)(2,1)S(1)} %fusion.18), channel_id=1, source_target_pairs={{0,8},{4,12},{8,0},{12,4},{16,24},{20,28},{24,16},{28,20},{1,9},{5... | collective-permute-start | bytes 393224 | tf_op jit(solution)/shard_map/ppermute | solution.py:205
  79.3 5.2 %collective-permute-start.25 = (bf16[2,16,2048]{2,1,0:T(8,128)(2,1)S(1)}, bf16[2,16,2048]{2,1,0:T(8,128)(2,1)S(1)}, u32[]{:S(2)}, u32[]{:S(2)}) collective-permute-start(bf16[2,16,2048]{2,1,0:T(8,128)(2,1)S(1)} %fusion.21), channel_id=1, source_target_pairs={{0,16},{4,20},{8,24},{12,28},{16,0},{20,4},{24,8},{28,12},{1,17},{... | collective-permute-start | bytes 393224 | tf_op jit(solution)/shard_map/ppermute | solution.py:205
  81.0 6.6 %collective-permute-start.19 = (bf16[2,16,2048]{2,1,0:T(8,128)(2,1)S(1)}, bf16[2,16,2048]{2,1,0:T(8,128)(2,1)S(1)}, u32[]{:S(2)}, u32[]{:S(2)}) collective-permute-start(bf16[2,16,2048]{2,1,0:T(8,128)(2,1)S(1)} %fusion.20), channel_id=1, source_target_pairs={{0,16},{4,20},{8,24},{12,28},{16,0},{20,4},{24,8},{28,12},{1,17},{... | collective-permute-start | bytes 393224 | tf_op jit(solution)/shard_map/ppermute | solution.py:205
  84.7 35.4 %collective-permute-start.28 = (bf16[16,2048]{1,0:T(8,128)(2,1)S(1)}, bf16[16,2048]{1,0:T(8,128)(2,1)S(1)}, u32[]{:S(2)}, u32[]{:S(2)}) collective-permute-start(bf16[16,2048]{1,0:T(8,128)(2,1)S(1)} %fusion.23), channel_id=1, source_target_pairs={{0,24},{4,28},{8,16},{12,20},{16,8},{20,12},{24,0},{28,4},{1,25},{... | collective-permute-start | bytes 196616 | tf_op jit(solution)/shard_map/ppermute | solution.py:205
  87.0 33.1 %collective-permute-start.27 = (bf16[16,2048]{1,0:T(8,128)(2,1)S(1)}, bf16[16,2048]{1,0:T(8,128)(2,1)S(1)}, u32[]{:S(2)}, u32[]{:S(2)}) collective-permute-start(bf16[16,2048]{1,0:T(8,128)(2,1)S(1)} %fusion.23), channel_id=1, source_target_pairs={{0,16},{4,20},{8,24},{12,28},{16,0},{20,4},{24,8},{28,12},{1,17},{... | collective-permute-start | bytes 196616 | tf_op jit(solution)/shard_map/ppermute | solution.py:205
  88.1 7.1 %collective-permute-start.7 = (bf16[2,32,2560]{2,1,0:T(8,128)(2,1)S(1)}, bf16[2,32,2560]{2,1,0:T(8,128)(2,1)S(1)}, u32[]{:S(2)}, u32[]{:S(2)}) collective-permute-start(bf16[2,32,2560]{2,1,0:T(8,128)(2,1)S(1)} %bitcast.160), channel_id=1, source_target_pairs={{0,8},{4,12},{8,0},{12,4},{16,24},{20,28},{24,16},{28,20},{1,9},{5... | collective-permute-start | bytes 983048 | tf_op jit(solution)/shard_map/ppermute | solution.py:205
  89.6 8.9 %collective-permute-start.16 = (bf16[2,32,2560]{2,1,0:T(8,128)(2,1)S(1)}, bf16[2,32,2560]{2,1,0:T(8,128)(2,1)S(1)}, u32[]{:S(2)}, u32[]{:S(2)}) collective-permute-start(bf16[2,32,2560]{2,1,0:T(8,128)(2,1)S(1)} %fusion.3), channel_id=1, source_target_pairs={{0,16},{4,20},{8,24},{12,28},{16,0},{20,4},{24,8},{28,12},{1,17},{... | collective-permute-start | bytes 983048 | tf_op jit(solution)/shard_map/ppermute | solution.py:205
  95.4 5.4 %collective-permute-start.8 = (bf16[2,16,2560]{2,1,0:T(8,128)(2,1)S(1)}, bf16[2,16,2560]{2,1,0:T(8,128)(2,1)S(1)}, u32[]{:S(2)}, u32[]{:S(2)}) collective-permute-start(bf16[2,16,2560]{2,1,0:T(8,128)(2,1)S(1)} %fusion.12), channel_id=1, source_target_pairs={{0,16},{4,20},{8,24},{12,28},{16,0},{20,4},{24,8},{28,12},{1,17},{... | collective-permute-start | bytes 491528 | tf_op jit(solution)/shard_map/ppermute | solution.py:205
  98.5 7.1 %collective-permute-start.17 = (bf16[2,16,2560]{2,1,0:T(8,128)(2,1)S(1)}, bf16[2,16,2560]{2,1,0:T(8,128)(2,1)S(1)}, u32[]{:S(2)}, u32[]{:S(2)}) collective-permute-start(bf16[2,16,2560]{2,1,0:T(8,128)(2,1)S(1)} %fusion.13), channel_id=1, source_target_pairs={{0,8},{4,12},{8,0},{12,4},{16,24},{20,28},{24,16},{28,20},{1,9},{5... | collective-permute-start | bytes 491528 | tf_op jit(solution)/shard_map/ppermute | solution.py:205
  100.9 10.3 %collective-permute-start.14 = (bf16[16,6656]{1,0:T(8,128)(2,1)S(1)}, bf16[16,6656]{1,0:T(8,128)(2,1)S(1)}, u32[]{:S(2)}, u32[]{:S(2)}) collective-permute-start(bf16[16,6656]{1,0:T(8,128)(2,1)S(1)} %pad_maximum_fusion.3), channel_id=1, source_target_pairs={{0,24},{4,28},{8,16},{12,20},{16,8},{20,12},{24,0},{28,4},{1,25},{... | collective-permute-start | bytes 638984 | tf_op jit(solution)/shard_map/ppermute | solution.py:205
  102.9 10.4 %collective-permute-start.13 = (bf16[16,6656]{1,0:T(8,128)(2,1)S(1)}, bf16[16,6656]{1,0:T(8,128)(2,1)S(1)}, u32[]{:S(2)}, u32[]{:S(2)}) collective-permute-start(bf16[16,6656]{1,0:T(8,128)(2,1)S(1)} %pad_maximum_fusion.3), channel_id=1, source_target_pairs={{0,16},{4,20},{8,24},{12,28},{16,0},{20,4},{24,8},{28,12},{1,17},{... | collective-permute-start | bytes 638984 | tf_op jit(solution)/shard_map/ppermute | solution.py:205
  105.7 9.1 %collective-permute-start.12 = (bf16[16,6656]{1,0:T(8,128)(2,1)S(1)}, bf16[16,6656]{1,0:T(8,128)(2,1)S(1)}, u32[]{:S(2)}, u32[]{:S(2)}) collective-permute-start(bf16[16,6656]{1,0:T(8,128)(2,1)S(1)} %pad_maximum_fusion.3), channel_id=1, source_target_pairs={{0,8},{4,12},{8,0},{12,4},{16,24},{20,28},{24,16},{28,20},{1,9},{5... | collective-permute-start | bytes 638984 | tf_op jit(solution)/shard_map/ppermute | solution.py:205
  111.2 6.9 %collective-permute-start.22 = (bf16[16,4608]{1,0:T(8,128)(2,1)S(1)}, bf16[16,4608]{1,0:T(8,128)(2,1)S(1)}, u32[]{:S(2)}, u32[]{:S(2)}) collective-permute-start(bf16[16,4608]{1,0:T(8,128)(2,1)S(1)} %pad_maximum_fusion.4), channel_id=1, source_target_pairs={{0,24},{4,28},{8,16},{12,20},{16,8},{20,12},{24,0},{28,4},{1,25},{... | collective-permute-start | bytes 442376 | tf_op jit(solution)/shard_map/ppermute | solution.py:205
  113.3 5.9 %collective-permute-start.21 = (bf16[16,4608]{1,0:T(8,128)(2,1)S(1)}, bf16[16,4608]{1,0:T(8,128)(2,1)S(1)}, u32[]{:S(2)}, u32[]{:S(2)}) collective-permute-start(bf16[16,4608]{1,0:T(8,128)(2,1)S(1)} %pad_maximum_fusion.4), channel_id=1, source_target_pairs={{0,16},{4,20},{8,24},{12,28},{16,0},{20,4},{24,8},{28,12},{1,17},{... | collective-permute-start | bytes 442376 | tf_op jit(solution)/shard_map/ppermute | solution.py:205
  114.8 5.1 %collective-permute-start.20 = (bf16[16,4608]{1,0:T(8,128)(2,1)S(1)}, bf16[16,4608]{1,0:T(8,128)(2,1)S(1)}, u32[]{:S(2)}, u32[]{:S(2)}) collective-permute-start(bf16[16,4608]{1,0:T(8,128)(2,1)S(1)} %pad_maximum_fusion.4), channel_id=1, source_target_pairs={{0,8},{4,12},{8,0},{12,4},{16,24},{20,28},{24,16},{28,20},{1,9},{5... | collective-permute-start | bytes 442376 | tf_op jit(solution)/shard_map/ppermute | solution.py:205
  119.2 24.2 %collective-permute-start.15 = (bf16[64,6656]{1,0:T(8,128)(2,1)S(1)}, bf16[64,6656]{1,0:T(8,128)(2,1)S(1)}, u32[]{:S(2)}, u32[]{:S(2)}) collective-permute-start(bf16[64,6656]{1,0:T(8,128)(2,1)S(1)} %pad_maximum_fusion.refs_0_), channel_id=1, source_target_pairs={{0,4},{4,0},{8,12},{12,8},{16,20},{20,16},{24,28},{28,24},{1,5},{5... | collective-permute-start | bytes 2555912 | tf_op jit(solution)/shard_map/ppermute | solution.py:205
  120.0 13.3 %collective-permute-start.23 = (bf16[64,4608]{1,0:T(8,128)(2,1)S(1)}, bf16[64,4608]{1,0:T(8,128)(2,1)S(1)}, u32[]{:S(2)}, u32[]{:S(2)}) collective-permute-start(bf16[64,4608]{1,0:T(8,128)(2,1)S(1)} %pad_maximum_fusion.1.refs_0_), channel_id=1, source_target_pairs={{0,4},{4,0},{8,12},{12,8},{16,20},{20,16},{24,28},{28,24},{1,5},{5... | collective-permute-start | bytes 1769480 | tf_op jit(solution)/shard_map/ppermute | solution.py:205
  122.4 8.9 %collective-permute-start.29 = (bf16[64,2048]{1,0:T(8,128)(2,1)S(1)}, bf16[64,2048]{1,0:T(8,128)(2,1)S(1)}, u32[]{:S(2)}, u32[]{:S(2)}) collective-permute-start(bf16[64,2048]{1,0:T(8,128)(2,1)S(1)} %pad_maximum_fusion.2.refs_0_), channel_id=1, source_target_pairs={{0,4},{4,0},{8,12},{12,8},{16,20},{20,16},{24,28},{28,24},{1,5},{5... | collective-permute-start | bytes 786440 | tf_op jit(solution)/shard_map/ppermute | solution.py:205
  137.0 11.3 %collective-permute-start.31 = (bf16[64,2048]{1,0:T(8,128)(2,1)S(1)}, bf16[64,2048]{1,0:T(8,128)(2,1)S(1)}, u32[]{:S(2)}, u32[]{:S(2)}) collective-permute-start(bf16[64,2048]{1,0:T(8,128)(2,1)S(1)} %get-tuple-element.37), channel_id=1, source_target_pairs={{0,3},{1,2},{2,1},{3,0},{4,7},{5,6},{6,5},{7,4},{8,11},{9,10},{10,... | collective-permute-start | bytes 786440 | tf_op jit(solution)/shard_map/ppermute | solution.py:208
  139.5 24.9 %collective-permute-start.30 = (bf16[64,2048]{1,0:T(8,128)(2,1)S(1)}, bf16[64,2048]{1,0:T(8,128)(2,1)S(1)}, u32[]{:S(2)}, u32[]{:S(2)}) collective-permute-start(bf16[64,2048]{1,0:T(8,128)(2,1)S(1)} %get-tuple-element.36), channel_id=1, source_target_pairs={{0,2},{1,3},{2,0},{3,1},{4,6},{5,7},{6,4},{7,5},{8,10},{9,11},{10,... | collective-permute-start | bytes 786440 | tf_op jit(solution)/shard_map/ppermute | solution.py:208
  148.1 16.3 %collective-permute-start.32 = (bf16[64,2048]{1,0:T(8,128)(2,1)S(1)}, bf16[64,2048]{1,0:T(8,128)(2,1)S(1)}, u32[]{:S(2)}, u32[]{:S(2)}) collective-permute-start(bf16[64,2048]{1,0:T(8,128)(2,1)S(1)} %get-tuple-element.38), channel_id=1, source_target_pairs={{0,1},{1,0},{2,3},{3,2},{4,5},{5,4},{6,7},{7,6},{8,9},{9,8},{10,11... | collective-permute-start | bytes 786440 | tf_op jit(solution)/shard_map/ppermute | solution.py:208
  (2 other events, 5.2 us)

commit v3 on v2

--- a/solution.py
+++ b/solution.py
@@ -101,18 +101,42 @@
     def kernel(x, g, u, keep, send):
         cols = pl.ds(pl.multiple_of(pl.program_id(0) * bn, bn), bn)
         for i, w in enumerate((g, u)):
-            tile = w[:, cols] if held[i] else w[...]
+            tile = w[:, cols]
             part = jnp.dot(x[...], tile, preferred_element_type=F32)
             keep[i] = part[:half]
             send[i] = part[half:].astype(send.dtype)
 
+    def deep(x, g, u, keep, send, buf, sems):
+        j = pl.program_id(0)
+
+        def copies(i):
+            cols = pl.ds(pl.multiple_of((first + i) * bn, bn), bn)
+            return [pltpu.make_async_copy(w.at[:, cols], buf.at[i, q], sems.at[i, q]) for q, w in enumerate((g, u))]
+
+        @pl.when(j == 0)
+        def _():
+            for i in range(min(3, n)):
+                for c in copies(i):
+                    c.start()
+
+        for q, c in enumerate(copies(j)):
+            c.wait()
+            part = jnp.dot(x[...], buf[j, q], preferred_element_type=F32)
+            keep[q] = part[:half]
+            send[q] = part[half:]
+
+        @pl.when(j + 3 < n)
+        def _():
+            for c in copies(j + 3):
+                c.start()
+
     o_spec = pl.BlockSpec((2, half, bn), lambda j: (0, 0, j))
-    stream = pl.BlockSpec((k, bn), lambda j: (0, first + j))
-    return pl.pallas_call(
-        kernel,
+    return pl.pallas_call(
+        kernel if all(held) else deep,
         grid=(n,),
         in_specs=[pl.BlockSpec((rows, k), lambda j: (0, 0))]
-        + [pl.BlockSpec(memory_space=pltpu.VMEM) if h else stream for h in held],
+        + [pl.BlockSpec(memory_space=pltpu.VMEM if all(held) else pl.ANY)] * 2,
+        scratch_shapes=[] if all(held) else [pltpu.VMEM((n, 2, k, bn), BF16), pltpu.SemaphoreType.DMA((n, 2))],
         out_specs=[o_spec, o_spec],
         out_shape=[
             jax.ShapeDtypeStruct((2, half, n * bn), F32),

time: 165 us -> 164 us (level)
  no operation moved by 1% of the time
where the time goes in v3:
time: 164 us
  waiting for transfers between devices  68.3 us (42%)
  Pallas kernels  51.6 us (31%)
  starting transfers between devices  38 us (23%)
  other arithmetic  4.22 us (3%)
    ppermute x6, waiting for transfers between devices, across(): return lax.ppermute(v, 'gy', [(i, i ^ mask) for i in range(nz)])  35 us
    ppermute x27, waiting for transfers between devices, swap(): return lax.ppermute(v, 'gx', [(i, i ^ mask) for i in range(nx)])  33.3 us
    ppermute x27, starting transfers between devices, swap(): return lax.ppermute(v, 'gx', [(i, i ^ mask) for i in range(nx)])  25.8 us
    pallas_call x3, Pallas kernels, gate_up(): pl.pallas_call(kernel if all(held) else deep, grid=(n,), in_specs=[pl.Blo...  20.2 us
    ppermute x6, starting transfers between devices, across(): return lax.ppermute(v, 'gy', [(i, i ^ mask) for i in range(nz)])  12.2 us
    pallas_call x1, Pallas kernels, fetch(): pl.pallas_call(kernel, in_specs=[pl.BlockSpec(memory_space=pl.ANY)] * len...  12 us
    pallas_call x3, Pallas kernels, down(): pl.pallas_call(kernel, grid_spec=pltpu.PrefetchScalarGridSpec(num_scalar_...  10.5 us
    pallas_call x1, Pallas kernels, fetch_rows(): pl.pallas_call(kernel, in_specs=[pl.BlockSpec(memory_space=pl.ANY)], out_...  8.78 us
  transfers between devices with their start and end apart: 33, of which 17 were waited for; matrix products, arithmetic and copies ran while one was open for 2% of the time, Pallas kernels for 26%

profile of v3, /device:TPU:0, one launch (start us, length us, event | category | flops | bytes accessed | tf_op | source)
XLA Modules:
  0.0 163.9 jit_solution(13250678480931942042)
XLA Ops:
  0.0 3.1 %collective-permute-start = (bf16[64,2048]{1,0:T(8,128)(2,1)}, bf16[64,2048]{1,0:T(8,128)(2,1)S(1)}, u32[]{:S(2)}, u32[]{:S(2)}) collective-permute-start(bf16[64,2048]{1,0:T(8,128)(2,1)} %refs_0_.2), channel_id=1, source_target_pairs={{0,1},{1,0},{2,3},{3,2},{4,5},{5,4},{6,7},{7,6},{8,9},{9,8},{10,11... | collective-permute-start | bytes 786440 | tf_op jit(solution)/shard_map/ppermute | solution.py:232
  3.1 2.6 %collective-permute-start.1 = (bf16[64,2048]{1,0:T(8,128)(2,1)}, bf16[64,2048]{1,0:T(8,128)(2,1)S(1)}, u32[]{:S(2)}, u32[]{:S(2)}) collective-permute-start(bf16[64,2048]{1,0:T(8,128)(2,1)} %refs_0_.2), channel_id=1, source_target_pairs={{0,2},{1,3},{2,0},{3,1},{4,6},{5,7},{6,4},{7,5},{8,10},{9,11},{10,... | collective-permute-start | bytes 786440 | tf_op jit(solution)/shard_map/ppermute | solution.py:232
  5.6 8.8 %collective-permute-done.refs_1_ = bf16[64,2048]{1,0:T(8,128)(2,1)S(1)} collective-permute-done((bf16[64,2048]{1,0:T(8,128)(2,1)}, bf16[64,2048]{1,0:T(8,128)(2,1)S(1)}, u32[]{:S(2)}, u32[]{:S(2)}) %collective-permute-start) | collective-permute-done | bytes 262176 | tf_op jit(solution)/shard_map/ppermute | solution.py:232
  14.4 10.1 %collective-permute-done.1.refs_2_ = bf16[64,2048]{1,0:T(8,128)(2,1)S(1)} collective-permute-done((bf16[64,2048]{1,0:T(8,128)(2,1)}, bf16[64,2048]{1,0:T(8,128)(2,1)S(1)}, u32[]{:S(2)}, u32[]{:S(2)}) %collective-permute-start.1) | collective-permute-done | bytes 262176 | tf_op jit(solution)/shard_map/ppermute | solution.py:232
  25.7 8.3 %shard_map.50 = (f32[2,128,2048]{2,1,0:T(8,128)S(1)}, f32[2,128,2048]{2,1,0:T(8,128)}) custom-call(bf16[256,2048]{1,0:T(8,128)(2,1)S(1)} %shard_map.46.x, bf16[2048,6656]{1,0:T(8,128)(2,1)} %g.1, bf16[2048,6656]{1,0:T(8,128)(2,1)} %u.1), custom_call_target="tpu_custom_call" | custom-call | flops 4294967296 | bytes 22020096 | tf_op jit(solution)/shard_map/pallas_call | solution.py:134
  34.1 12.0 %shard_map.47 = (bf16[2048,2048]{1,0:T(8,128)(2,1)S(1)}, bf16[2048,2048]{1,0:T(8,128)(2,1)S(1)}, bf16[2048,2560]{1,0:T(8,128)(2,1)S(1)}, bf16[2048,2560]{1,0:T(8,128)(2,1)S(1)}) custom-call(bf16[2048,6656]{1,0:T(8,128)(2,1)} %g.1, bf16[2048,6656]{1,0:T(8,128)(2,1)} %u.1), custom_call_target="tpu_custom_call" | custom-call | bytes 54525952 | tf_op jit(solution)/shard_map/pallas_call | solution.py:86
  46.1 5.3 %shard_map.48 = (f32[2,128,2048]{2,1,0:T(8,128)S(1)}, f32[2,128,2048]{2,1,0:T(8,128)S(1)}) custom-call(bf16[256,2048]{1,0:T(8,128)(2,1)S(1)} %shard_map.46.x, bf16[2048,2048]{1,0:T(8,128)(2,1)S(1)} %get-tuple-element.22.g, bf16[2048,2048]{1,0:T(8,128)(2,1)S(1)} %get-tuple-element.23.u), custom_call_target="tpu_custom_call" | custom-call | flops 4294967296 | bytes 22020096 | tf_op jit(solution)/shard_map/pallas_call | solution.py:134
  51.9 6.5 %shard_map.49 = (f32[2,128,2560]{2,1,0:T(8,128)S(1)}, f32[2,128,2560]{2,1,0:T(8,128)S(1)}) custom-call(bf16[256,2048]{1,0:T(8,128)(2,1)S(1)} %shard_map.46.x, bf16[2048,2560]{1,0:T(8,128)(2,1)S(1)} %get-tuple-element.26.g, bf16[2048,2560]{1,0:T(8,128)(2,1)S(1)} %get-tuple-element.27.u), custom_call_target="tpu_custom_call" | custom-call | flops 5368709120 | bytes 27262976 | tf_op jit(solution)/shard_map/pallas_call | solution.py:134
  59.0 1.8 %slice_add_fusion.2 = (f32[2,64,2048]{2,1,0:T(8,128)S(1)}, f32[2,64,2048]{2,1,0:T(8,128)S(1)}) fusion(f32[2,128,2048]{2,1,0:T(8,128)} %collective-permute-done.3, f32[2,128,2048]{2,1,0:T(8,128)S(1)} %get-tuple-element.24), kind=kLoop, calls=%fused_computation.2 | loop fusion | flops 524288 | bytes 6291456 | tf_op jit(solution)/shard_map/add | solution.py:258
  60.9 1.6 collective-permute-start.10
  65.2 5.0 %collective-permute-done.10 = bf16[2,32,2048]{2,1,0:T(8,128)(2,1)S(1)} collective-permute-done((bf16[2,32,2048]{2,1,0:T(8,128)(2,1)S(1)}, bf16[2,32,2048]{2,1,0:T(8,128)(2,1)S(1)}, u32[]{:S(2)}, u32[]{:S(2)}) %collective-permute-start.10) | collective-permute-done | bytes 262176 | tf_op jit(solution)/shard_map/ppermute | solution.py:229
  70.3 1.6 collective-permute-start.11
  71.8 3.5 %collective-permute-done.4 = bf16[2,32,2048]{2,1,0:T(8,128)(2,1)S(1)} collective-permute-done((bf16[2,32,2048]{2,1,0:T(8,128)(2,1)S(1)}, bf16[2,32,2048]{2,1,0:T(8,128)(2,1)S(1)}, u32[]{:S(2)}, u32[]{:S(2)}) %collective-permute-start.4) | collective-permute-done | bytes 262176 | tf_op jit(solution)/shard_map/ppermute | solution.py:229
  75.4 1.6 collective-permute-start.5
  78.0 1.6 collective-permute-start.25
  80.3 3.0 %collective-permute-done.25 = bf16[2,16,2048]{2,1,0:T(8,128)(2,1)S(1)} collective-permute-done((bf16[2,16,2048]{2,1,0:T(8,128)(2,1)S(1)}, bf16[2,16,2048]{2,1,0:T(8,128)(2,1)S(1)}, u32[]{:S(2)}, u32[]{:S(2)}) %collective-permute-start.25) | collective-permute-done | bytes 131104 | tf_op jit(solution)/shard_map/ppermute | solution.py:229
  83.3 2.3 %collective-permute-start.28 = (bf16[16,2048]{1,0:T(8,128)(2,1)S(1)}, bf16[16,2048]{1,0:T(8,128)(2,1)S(1)}, u32[]{:S(2)}, u32[]{:S(2)}) collective-permute-start(bf16[16,2048]{1,0:T(8,128)(2,1)S(1)} %fusion.23), channel_id=1, source_target_pairs={{0,24},{4,28},{8,16},{12,20},{16,8},{20,12},{24,0},{28,4},{1,25},{... | collective-permute-start | bytes 196616 | tf_op jit(solution)/shard_map/ppermute | solution.py:229
  89.5 4.4 %collective-permute-done.7 = bf16[2,32,2560]{2,1,0:T(8,128)(2,1)S(1)} collective-permute-done((bf16[2,32,2560]{2,1,0:T(8,128)(2,1)S(1)}, bf16[2,32,2560]{2,1,0:T(8,128)(2,1)S(1)}, u32[]{:S(2)}, u32[]{:S(2)}) %collective-permute-start.7) | collective-permute-done | bytes 327712 | tf_op jit(solution)/shard_map/ppermute | solution.py:229
  94.0 1.6 collective-permute-start.8
  95.6 1.5 collective-permute-done.16
  99.5 2.0 %collective-permute-start.14 = (bf16[16,6656]{1,0:T(8,128)(2,1)S(1)}, bf16[16,6656]{1,0:T(8,128)(2,1)S(1)}, u32[]{:S(2)}, u32[]{:S(2)}) collective-permute-start(bf16[16,6656]{1,0:T(8,128)(2,1)S(1)} %pad_maximum_fusion.3), channel_id=1, source_target_pairs={{0,24},{4,28},{8,16},{12,20},{16,8},{20,12},{24,0},{28,4},{1,25},{... | collective-permute-start | bytes 638984 | tf_op jit(solution)/shard_map/ppermute | solution.py:229
  102.3 2.0 %collective-permute-done.17 = bf16[2,16,2560]{2,1,0:T(8,128)(2,1)S(1)} collective-permute-done((bf16[2,16,2560]{2,1,0:T(8,128)(2,1)S(1)}, bf16[2,16,2560]{2,1,0:T(8,128)(2,1)S(1)}, u32[]{:S(2)}, u32[]{:S(2)}) %collective-permute-start.17) | collective-permute-done | bytes 163872 | tf_op jit(solution)/shard_map/ppermute | solution.py:229
  105.5 4.4 %collective-permute-done.14 = bf16[16,6656]{1,0:T(8,128)(2,1)S(1)} collective-permute-done((bf16[16,6656]{1,0:T(8,128)(2,1)S(1)}, bf16[16,6656]{1,0:T(8,128)(2,1)S(1)}, u32[]{:S(2)}, u32[]{:S(2)}) %collective-permute-start.14) | collective-permute-done | bytes 213024 | tf_op jit(solution)/shard_map/ppermute | solution.py:229
  114.6 2.2 %collective-permute-done.22 = bf16[16,4608]{1,0:T(8,128)(2,1)S(1)} collective-permute-done((bf16[16,4608]{1,0:T(8,128)(2,1)S(1)}, bf16[16,4608]{1,0:T(8,128)(2,1)S(1)}, u32[]{:S(2)}, u32[]{:S(2)}) %collective-permute-start.22) | collective-permute-done | bytes 147488 | tf_op jit(solution)/shard_map/ppermute | solution.py:229
  118.8 2.2 %collective-permute-done.26 = bf16[16,2048]{1,0:T(8,128)(2,1)S(1)} collective-permute-done((bf16[16,2048]{1,0:T(8,128)(2,1)S(1)}, bf16[16,2048]{1,0:T(8,128)(2,1)S(1)}, u32[]{:S(2)}, u32[]{:S(2)}) %collective-permute-start.26) | collective-permute-done | bytes 65568 | tf_op jit(solution)/shard_map/ppermute | solution.py:229
  121.1 8.8 %shard_map.51 = (bf16[2048,2048]{1,0:T(8,128)(2,1)S(1)}, bf16[2560,2048]{1,0:T(8,128)(2,1)S(1)}, bf16[2048,2048]{1,0:T(8,128)(2,1)S(1)}) custom-call(bf16[6656,2048]{1,0:T(8,128)(2,1)} %w.1), custom_call_target="tpu_custom_call" | custom-call | bytes 54525952 | tf_op jit(solution)/shard_map/pallas_call | solution.py:166
  129.9 2.0 %shard_map.53.refs_4_ = f32[128,2048]{1,0:T(8,128)S(1)} custom-call(s32[1]{0:T(128)} %bitcast.me_ref, bf16[64,2048]{1,0:T(8,128)(2,1)S(1)} %pad_maximum_fusion.2.refs_0_, bf16[64,2048]{1,0:T(8,128)(2,1)S(1)} %collective-permute-done.29.refs_1_, bf16[2048,2048]{1,0:T(8,128)(2,1)S(1)} %get-tuple-element.32.refs_2_), custom_call_target="tpu_custom_call" | custom-call | flops 1073741824 | bytes 9961472 | tf_op jit(solution)/shard_map/pallas_call | solution.py:212
  132.0 3.7 %shard_map.54 = (bf16[64,2048]{1,0:T(8,128)(2,1)S(1)}, bf16[64,2048]{1,0:T(8,128)(2,1)S(1)}) custom-call(s32[1]{0:T(128)} %bitcast.me_ref, bf16[64,4608]{1,0:T(8,128)(2,1)S(1)} %pad_maximum_fusion.1.refs_0_, bf16[64,4608]{1,0:T(8,128)(2,1)S(1)} %collective-permute-done.23.refs_1_, bf16[2560,2048]{1,0:T(8,128)(2,1)S(1)} %get-tuple-element.33.refs_3_.refs_2_, ...), custom_call_target="tpu_custom_call" | custom-call | flops 2415919104 | bytes 21102592 | tf_op jit(solution)/shard_map/pallas_call | solution.py:212
  135.7 2.5 %collective-permute-start.31 = (bf16[64,2048]{1,0:T(8,128)(2,1)S(1)}, bf16[64,2048]{1,0:T(8,128)(2,1)S(1)}, u32[]{:S(2)}, u32[]{:S(2)}) collective-permute-start(bf16[64,2048]{1,0:T(8,128)(2,1)S(1)} %get-tuple-element.37), channel_id=1, source_target_pairs={{0,3},{1,2},{2,1},{3,0},{4,7},{5,6},{6,5},{7,4},{8,11},{9,10},{10,... | collective-permute-start | bytes 786440 | tf_op jit(solution)/shard_map/ppermute | solution.py:232
  138.2 3.8 %collective-permute-start.30 = (bf16[64,2048]{1,0:T(8,128)(2,1)S(1)}, bf16[64,2048]{1,0:T(8,128)(2,1)S(1)}, u32[]{:S(2)}, u32[]{:S(2)}) collective-permute-start(bf16[64,2048]{1,0:T(8,128)(2,1)S(1)} %get-tuple-element.36), channel_id=1, source_target_pairs={{0,2},{1,3},{2,0},{3,1},{4,6},{5,7},{6,4},{7,5},{8,10},{9,11},{10,... | collective-permute-start | bytes 786440 | tf_op jit(solution)/shard_map/ppermute | solution.py:232
  142.0 4.8 %shard_map.52 = (f32[64,2048]{1,0:T(8,128)S(1)}, bf16[64,2048]{1,0:T(8,128)(2,1)S(1)}) custom-call(s32[1]{0:T(128)} %bitcast.me_ref, bf16[64,6656]{1,0:T(8,128)(2,1)S(1)} %pad_maximum_fusion.refs_0_, bf16[64,6656]{1,0:T(8,128)(2,1)S(1)} %collective-permute-done.15.refs_1_, bf16[2048,2048]{1,0:T(8,128)(2,1)S(1)} %get-tuple-element.32.refs_2_, ...), custom_call_target="tpu_custom_call" | custom-call | flops 3489660928 | bytes 30015488 | tf_op jit(solution)/shard_map/pallas_call | solution.py:212
  147.0 16.1 %collective-permute-done.30 = bf16[64,2048]{1,0:T(8,128)(2,1)S(1)} collective-permute-done((bf16[64,2048]{1,0:T(8,128)(2,1)S(1)}, bf16[64,2048]{1,0:T(8,128)(2,1)S(1)}, u32[]{:S(2)}, u32[]{:S(2)}) %collective-permute-start.30) | collective-permute-done | bytes 262176 | tf_op jit(solution)/shard_map/ppermute | solution.py:232
  (87 shorter events, 22.8 us)
Async XLA Ops:
  0.0 14.4 %collective-permute-start = (bf16[64,2048]{1,0:T(8,128)(2,1)}, bf16[64,2048]{1,0:T(8,128)(2,1)S(1)}, u32[]{:S(2)}, u32[]{:S(2)}) collective-permute-start(bf16[64,2048]{1,0:T(8,128)(2,1)} %refs_0_.2), channel_id=1, source_target_pairs={{0,1},{1,0},{2,3},{3,2},{4,5},{5,4},{6,7},{7,6},{8,9},{9,8},{10,11... | collective-permute-start | bytes 786440 | tf_op jit(solution)/shard_map/ppermute | solution.py:232
  3.1 21.5 %collective-permute-start.1 = (bf16[64,2048]{1,0:T(8,128)(2,1)}, bf16[64,2048]{1,0:T(8,128)(2,1)S(1)}, u32[]{:S(2)}, u32[]{:S(2)}) collective-permute-start(bf16[64,2048]{1,0:T(8,128)(2,1)} %refs_0_.2), channel_id=1, source_target_pairs={{0,2},{1,3},{2,0},{3,1},{4,6},{5,7},{6,4},{7,5},{8,10},{9,11},{10,... | collective-permute-start | bytes 786440 | tf_op jit(solution)/shard_map/ppermute | solution.py:232
  5.6 18.9 %collective-permute-start.2 = (bf16[64,2048]{1,0:T(8,128)(2,1)}, bf16[64,2048]{1,0:T(8,128)(2,1)S(1)}, u32[]{:S(2)}, u32[]{:S(2)}) collective-permute-start(bf16[64,2048]{1,0:T(8,128)(2,1)} %refs_0_.2), channel_id=1, source_target_pairs={{0,3},{1,2},{2,1},{3,0},{4,7},{5,6},{6,5},{7,4},{8,11},{9,10},{10,... | collective-permute-start | bytes 786440 | tf_op jit(solution)/shard_map/ppermute | solution.py:232
  34.0 24.6 %collective-permute-start.9 = (f32[2,128,2048]{2,1,0:T(8,128)}, f32[2,128,2048]{2,1,0:T(8,128)S(1)}, u32[]{:S(2)}, u32[]{:S(2)}) collective-permute-start(f32[2,128,2048]{2,1,0:T(8,128)} %get-tuple-element.31), channel_id=1, source_target_pairs={{0,4},{4,0},{8,12},{12,8},{16,20},{20,16},{24,28},{28,24},{1,5},{5... | collective-permute-start | bytes 6291464 | tf_op jit(solution)/shard_map/ppermute | solution.py:229
  51.4 7.6 %collective-permute-start.3 = (f32[2,128,2048]{2,1,0:T(8,128)S(1)}, f32[2,128,2048]{2,1,0:T(8,128)}, u32[]{:S(2)}, u32[]{:S(2)}) collective-permute-start(f32[2,128,2048]{2,1,0:T(8,128)S(1)} %get-tuple-element.25), channel_id=1, source_target_pairs={{0,4},{4,0},{8,12},{12,8},{16,20},{20,16},{24,28},{28,24},{1,5},{5... | collective-permute-start | bytes 6291464 | tf_op jit(solution)/shard_map/ppermute | solution.py:229
  58.5 27.9 %collective-permute-start.6 = (f32[2,128,2560]{2,1,0:T(8,128)S(1)}, f32[2,128,2560]{2,1,0:T(8,128)S(1)}, u32[]{:S(2)}, u32[]{:S(2)}) collective-permute-start(f32[2,128,2560]{2,1,0:T(8,128)S(1)} %get-tuple-element.29), channel_id=1, source_target_pairs={{0,4},{4,0},{8,12},{12,8},{16,20},{20,16},{24,28},{28,24},{1,5},{5... | collective-permute-start | bytes 7864328 | tf_op jit(solution)/shard_map/ppermute | solution.py:229
  60.9 9.2 %collective-permute-start.10 = (bf16[2,32,2048]{2,1,0:T(8,128)(2,1)S(1)}, bf16[2,32,2048]{2,1,0:T(8,128)(2,1)S(1)}, u32[]{:S(2)}, u32[]{:S(2)}) collective-permute-start(bf16[2,32,2048]{2,1,0:T(8,128)(2,1)S(1)} %fusion.7), channel_id=1, source_target_pairs={{0,16},{4,20},{8,24},{12,28},{16,0},{20,4},{24,8},{28,12},{1,17},{... | collective-permute-start | bytes 786440 | tf_op jit(solution)/shard_map/ppermute | solution.py:229
  62.6 12.8 %collective-permute-start.4 = (bf16[2,32,2048]{2,1,0:T(8,128)(2,1)S(1)}, bf16[2,32,2048]{2,1,0:T(8,128)(2,1)S(1)}, u32[]{:S(2)}, u32[]{:S(2)}) collective-permute-start(bf16[2,32,2048]{2,1,0:T(8,128)(2,1)S(1)} %fusion.6), channel_id=1, source_target_pairs={{0,16},{4,20},{8,24},{12,28},{16,0},{20,4},{24,8},{28,12},{1,17},{... | collective-permute-start | bytes 786440 | tf_op jit(solution)/shard_map/ppermute | solution.py:229
  63.1 16.5 %collective-permute-start.18 = (bf16[2,32,2048]{2,1,0:T(8,128)(2,1)S(1)}, bf16[2,32,2048]{2,1,0:T(8,128)(2,1)S(1)}, u32[]{:S(2)}, u32[]{:S(2)}) collective-permute-start(bf16[2,32,2048]{2,1,0:T(8,128)(2,1)S(1)} %bitcast.161), channel_id=1, source_target_pairs={{0,8},{4,12},{8,0},{12,4},{16,24},{20,28},{24,16},{28,20},{1,9},{5... | collective-permute-start | bytes 786440 | tf_op jit(solution)/shard_map/ppermute | solution.py:229
  64.6 13.3 %collective-permute-start.24 = (bf16[2,32,2048]{2,1,0:T(8,128)(2,1)S(1)}, bf16[2,32,2048]{2,1,0:T(8,128)(2,1)S(1)}, u32[]{:S(2)}, u32[]{:S(2)}) collective-permute-start(bf16[2,32,2048]{2,1,0:T(8,128)(2,1)S(1)} %bitcast.162), channel_id=1, source_target_pairs={{0,8},{4,12},{8,0},{12,4},{16,24},{20,28},{24,16},{28,20},{1,9},{5... | collective-permute-start | bytes 786440 | tf_op jit(solution)/shard_map/ppermute | solution.py:229
  70.3 15.4 %collective-permute-start.11 = (bf16[2,16,2048]{2,1,0:T(8,128)(2,1)S(1)}, bf16[2,16,2048]{2,1,0:T(8,128)(2,1)S(1)}, u32[]{:S(2)}, u32[]{:S(2)}) collective-permute-start(bf16[2,16,2048]{2,1,0:T(8,128)(2,1)S(1)} %fusion.19), channel_id=1, source_target_pairs={{0,8},{4,12},{8,0},{12,4},{16,24},{20,28},{24,16},{28,20},{1,9},{5... | collective-permute-start | bytes 393224 | tf_op jit(solution)/shard_map/ppermute | solution.py:229
  75.4 10.8 %collective-permute-start.5 = (bf16[2,16,2048]{2,1,0:T(8,128)(2,1)S(1)}, bf16[2,16,2048]{2,1,0:T(8,128)(2,1)S(1)}, u32[]{:S(2)}, u32[]{:S(2)}) collective-permute-start(bf16[2,16,2048]{2,1,0:T(8,128)(2,1)S(1)} %fusion.18), channel_id=1, source_target_pairs={{0,8},{4,12},{8,0},{12,4},{16,24},{20,28},{24,16},{28,20},{1,9},{5... | collective-permute-start | bytes 393224 | tf_op jit(solution)/shard_map/ppermute | solution.py:229
  78.0 5.2 %collective-permute-start.25 = (bf16[2,16,2048]{2,1,0:T(8,128)(2,1)S(1)}, bf16[2,16,2048]{2,1,0:T(8,128)(2,1)S(1)}, u32[]{:S(2)}, u32[]{:S(2)}) collective-permute-start(bf16[2,16,2048]{2,1,0:T(8,128)(2,1)S(1)} %fusion.21), channel_id=1, source_target_pairs={{0,16},{4,20},{8,24},{12,28},{16,0},{20,4},{24,8},{28,12},{1,17},{... | collective-permute-start | bytes 393224 | tf_op jit(solution)/shard_map/ppermute | solution.py:229
  79.7 6.6 %collective-permute-start.19 = (bf16[2,16,2048]{2,1,0:T(8,128)(2,1)S(1)}, bf16[2,16,2048]{2,1,0:T(8,128)(2,1)S(1)}, u32[]{:S(2)}, u32[]{:S(2)}) collective-permute-start(bf16[2,16,2048]{2,1,0:T(8,128)(2,1)S(1)} %fusion.20), channel_id=1, source_target_pairs={{0,16},{4,20},{8,24},{12,28},{16,0},{20,4},{24,8},{28,12},{1,17},{... | collective-permute-start | bytes 393224 | tf_op jit(solution)/shard_map/ppermute | solution.py:229
  83.3 35.4 %collective-permute-start.28 = (bf16[16,2048]{1,0:T(8,128)(2,1)S(1)}, bf16[16,2048]{1,0:T(8,128)(2,1)S(1)}, u32[]{:S(2)}, u32[]{:S(2)}) collective-permute-start(bf16[16,2048]{1,0:T(8,128)(2,1)S(1)} %fusion.23), channel_id=1, source_target_pairs={{0,24},{4,28},{8,16},{12,20},{16,8},{20,12},{24,0},{28,4},{1,25},{... | collective-permute-start | bytes 196616 | tf_op jit(solution)/shard_map/ppermute | solution.py:229
  85.6 33.1 %collective-permute-start.27 = (bf16[16,2048]{1,0:T(8,128)(2,1)S(1)}, bf16[16,2048]{1,0:T(8,128)(2,1)S(1)}, u32[]{:S(2)}, u32[]{:S(2)}) collective-permute-start(bf16[16,2048]{1,0:T(8,128)(2,1)S(1)} %fusion.23), channel_id=1, source_target_pairs={{0,16},{4,20},{8,24},{12,28},{16,0},{20,4},{24,8},{28,12},{1,17},{... | collective-permute-start | bytes 196616 | tf_op jit(solution)/shard_map/ppermute | solution.py:229
  86.8 7.1 %collective-permute-start.7 = (bf16[2,32,2560]{2,1,0:T(8,128)(2,1)S(1)}, bf16[2,32,2560]{2,1,0:T(8,128)(2,1)S(1)}, u32[]{:S(2)}, u32[]{:S(2)}) collective-permute-start(bf16[2,32,2560]{2,1,0:T(8,128)(2,1)S(1)} %bitcast.160), channel_id=1, source_target_pairs={{0,8},{4,12},{8,0},{12,4},{16,24},{20,28},{24,16},{28,20},{1,9},{5... | collective-permute-start | bytes 983048 | tf_op jit(solution)/shard_map/ppermute | solution.py:229
  88.2 8.9 %collective-permute-start.16 = (bf16[2,32,2560]{2,1,0:T(8,128)(2,1)S(1)}, bf16[2,32,2560]{2,1,0:T(8,128)(2,1)S(1)}, u32[]{:S(2)}, u32[]{:S(2)}) collective-permute-start(bf16[2,32,2560]{2,1,0:T(8,128)(2,1)S(1)} %fusion.3), channel_id=1, source_target_pairs={{0,16},{4,20},{8,24},{12,28},{16,0},{20,4},{24,8},{28,12},{1,17},{... | collective-permute-start | bytes 983048 | tf_op jit(solution)/shard_map/ppermute | solution.py:229
  94.0 5.4 %collective-permute-start.8 = (bf16[2,16,2560]{2,1,0:T(8,128)(2,1)S(1)}, bf16[2,16,2560]{2,1,0:T(8,128)(2,1)S(1)}, u32[]{:S(2)}, u32[]{:S(2)}) collective-permute-start(bf16[2,16,2560]{2,1,0:T(8,128)(2,1)S(1)} %fusion.12), channel_id=1, source_target_pairs={{0,16},{4,20},{8,24},{12,28},{16,0},{20,4},{24,8},{28,12},{1,17},{... | collective-permute-start | bytes 491528 | tf_op jit(solution)/shard_map/ppermute | solution.py:229
  97.2 7.1 %collective-permute-start.17 = (bf16[2,16,2560]{2,1,0:T(8,128)(2,1)S(1)}, bf16[2,16,2560]{2,1,0:T(8,128)(2,1)S(1)}, u32[]{:S(2)}, u32[]{:S(2)}) collective-permute-start(bf16[2,16,2560]{2,1,0:T(8,128)(2,1)S(1)} %fusion.13), channel_id=1, source_target_pairs={{0,8},{4,12},{8,0},{12,4},{16,24},{20,28},{24,16},{28,20},{1,9},{5... | collective-permute-start | bytes 491528 | tf_op jit(solution)/shard_map/ppermute | solution.py:229
  99.5 10.3 %collective-permute-start.14 = (bf16[16,6656]{1,0:T(8,128)(2,1)S(1)}, bf16[16,6656]{1,0:T(8,128)(2,1)S(1)}, u32[]{:S(2)}, u32[]{:S(2)}) collective-permute-start(bf16[16,6656]{1,0:T(8,128)(2,1)S(1)} %pad_maximum_fusion.3), channel_id=1, source_target_pairs={{0,24},{4,28},{8,16},{12,20},{16,8},{20,12},{24,0},{28,4},{1,25},{... | collective-permute-start | bytes 638984 | tf_op jit(solution)/shard_map/ppermute | solution.py:229
  101.6 10.4 %collective-permute-start.13 = (bf16[16,6656]{1,0:T(8,128)(2,1)S(1)}, bf16[16,6656]{1,0:T(8,128)(2,1)S(1)}, u32[]{:S(2)}, u32[]{:S(2)}) collective-permute-start(bf16[16,6656]{1,0:T(8,128)(2,1)S(1)} %pad_maximum_fusion.3), channel_id=1, source_target_pairs={{0,16},{4,20},{8,24},{12,28},{16,0},{20,4},{24,8},{28,12},{1,17},{... | collective-permute-start | bytes 638984 | tf_op jit(solution)/shard_map/ppermute | solution.py:229
  104.3 9.1 %collective-permute-start.12 = (bf16[16,6656]{1,0:T(8,128)(2,1)S(1)}, bf16[16,6656]{1,0:T(8,128)(2,1)S(1)}, u32[]{:S(2)}, u32[]{:S(2)}) collective-permute-start(bf16[16,6656]{1,0:T(8,128)(2,1)S(1)} %pad_maximum_fusion.3), channel_id=1, source_target_pairs={{0,8},{4,12},{8,0},{12,4},{16,24},{20,28},{24,16},{28,20},{1,9},{5... | collective-permute-start | bytes 638984 | tf_op jit(solution)/shard_map/ppermute | solution.py:229
  109.8 6.9 %collective-permute-start.22 = (bf16[16,4608]{1,0:T(8,128)(2,1)S(1)}, bf16[16,4608]{1,0:T(8,128)(2,1)S(1)}, u32[]{:S(2)}, u32[]{:S(2)}) collective-permute-start(bf16[16,4608]{1,0:T(8,128)(2,1)S(1)} %pad_maximum_fusion.4), channel_id=1, source_target_pairs={{0,24},{4,28},{8,16},{12,20},{16,8},{20,12},{24,0},{28,4},{1,25},{... | collective-permute-start | bytes 442376 | tf_op jit(solution)/shard_map/ppermute | solution.py:229
  112.0 5.9 %collective-permute-start.21 = (bf16[16,4608]{1,0:T(8,128)(2,1)S(1)}, bf16[16,4608]{1,0:T(8,128)(2,1)S(1)}, u32[]{:S(2)}, u32[]{:S(2)}) collective-permute-start(bf16[16,4608]{1,0:T(8,128)(2,1)S(1)} %pad_maximum_fusion.4), channel_id=1, source_target_pairs={{0,16},{4,20},{8,24},{12,28},{16,0},{20,4},{24,8},{28,12},{1,17},{... | collective-permute-start | bytes 442376 | tf_op jit(solution)/shard_map/ppermute | solution.py:229
  113.5 5.1 %collective-permute-start.20 = (bf16[16,4608]{1,0:T(8,128)(2,1)S(1)}, bf16[16,4608]{1,0:T(8,128)(2,1)S(1)}, u32[]{:S(2)}, u32[]{:S(2)}) collective-permute-start(bf16[16,4608]{1,0:T(8,128)(2,1)S(1)} %pad_maximum_fusion.4), channel_id=1, source_target_pairs={{0,8},{4,12},{8,0},{12,4},{16,24},{20,28},{24,16},{28,20},{1,9},{5... | collective-permute-start | bytes 442376 | tf_op jit(solution)/shard_map/ppermute | solution.py:229
  117.8 24.2 %collective-permute-start.15 = (bf16[64,6656]{1,0:T(8,128)(2,1)S(1)}, bf16[64,6656]{1,0:T(8,128)(2,1)S(1)}, u32[]{:S(2)}, u32[]{:S(2)}) collective-permute-start(bf16[64,6656]{1,0:T(8,128)(2,1)S(1)} %pad_maximum_fusion.refs_0_), channel_id=1, source_target_pairs={{0,4},{4,0},{8,12},{12,8},{16,20},{20,16},{24,28},{28,24},{1,5},{5... | collective-permute-start | bytes 2555912 | tf_op jit(solution)/shard_map/ppermute | solution.py:229
  118.7 13.3 %collective-permute-start.23 = (bf16[64,4608]{1,0:T(8,128)(2,1)S(1)}, bf16[64,4608]{1,0:T(8,128)(2,1)S(1)}, u32[]{:S(2)}, u32[]{:S(2)}) collective-permute-start(bf16[64,4608]{1,0:T(8,128)(2,1)S(1)} %pad_maximum_fusion.1.refs_0_), channel_id=1, source_target_pairs={{0,4},{4,0},{8,12},{12,8},{16,20},{20,16},{24,28},{28,24},{1,5},{5... | collective-permute-start | bytes 1769480 | tf_op jit(solution)/shard_map/ppermute | solution.py:229
  121.0 8.9 %collective-permute-start.29 = (bf16[64,2048]{1,0:T(8,128)(2,1)S(1)}, bf16[64,2048]{1,0:T(8,128)(2,1)S(1)}, u32[]{:S(2)}, u32[]{:S(2)}) collective-permute-start(bf16[64,2048]{1,0:T(8,128)(2,1)S(1)} %pad_maximum_fusion.2.refs_0_), channel_id=1, source_target_pairs={{0,4},{4,0},{8,12},{12,8},{16,20},{20,16},{24,28},{28,24},{1,5},{5... | collective-permute-start | bytes 786440 | tf_op jit(solution)/shard_map/ppermute | solution.py:229
  135.7 11.3 %collective-permute-start.31 = (bf16[64,2048]{1,0:T(8,128)(2,1)S(1)}, bf16[64,2048]{1,0:T(8,128)(2,1)S(1)}, u32[]{:S(2)}, u32[]{:S(2)}) collective-permute-start(bf16[64,2048]{1,0:T(8,128)(2,1)S(1)} %get-tuple-element.37), channel_id=1, source_target_pairs={{0,3},{1,2},{2,1},{3,0},{4,7},{5,6},{6,5},{7,4},{8,11},{9,10},{10,... | collective-permute-start | bytes 786440 | tf_op jit(solution)/shard_map/ppermute | solution.py:232
  138.2 24.9 %collective-permute-start.30 = (bf16[64,2048]{1,0:T(8,128)(2,1)S(1)}, bf16[64,2048]{1,0:T(8,128)(2,1)S(1)}, u32[]{:S(2)}, u32[]{:S(2)}) collective-permute-start(bf16[64,2048]{1,0:T(8,128)(2,1)S(1)} %get-tuple-element.36), channel_id=1, source_target_pairs={{0,2},{1,3},{2,0},{3,1},{4,6},{5,7},{6,4},{7,5},{8,10},{9,11},{10,... | collective-permute-start | bytes 786440 | tf_op jit(solution)/shard_map/ppermute | solution.py:232
  146.8 16.3 %collective-permute-start.32 = (bf16[64,2048]{1,0:T(8,128)(2,1)S(1)}, bf16[64,2048]{1,0:T(8,128)(2,1)S(1)}, u32[]{:S(2)}, u32[]{:S(2)}) collective-permute-start(bf16[64,2048]{1,0:T(8,128)(2,1)S(1)} %get-tuple-element.38), channel_id=1, source_target_pairs={{0,1},{1,0},{2,3},{3,2},{4,5},{5,4},{6,7},{7,6},{8,9},{9,8},{10,11... | collective-permute-start | bytes 786440 | tf_op jit(solution)/shard_map/ppermute | solution.py:232
  (2 other events, 5.2 us)

commit v4 on v3

--- a/solution.py
+++ b/solution.py
@@ -115,7 +115,7 @@
 
         @pl.when(j == 0)
         def _():
-            for i in range(min(3, n)):
+            for i in range(min(4, n)):
                 for c in copies(i):
                     c.start()
 
@@ -125,9 +125,9 @@
             keep[q] = part[:half]
             send[q] = part[half:]
 
-        @pl.when(j + 3 < n)
+        @pl.when(j + 4 < n)
         def _():
-            for c in copies(j + 3):
+            for c in copies(j + 4):
                 c.start()
 
     o_spec = pl.BlockSpec((2, half, bn), lambda j: (0, 0, j))

time: 164 us -> 164 us (level)
  no operation moved by 1% of the time
where the time goes in v4:
time: 164 us
  waiting for transfers between devices  68.3 us (42%)
  Pallas kernels  51.6 us (31%)
  starting transfers between devices  38 us (23%)
  other arithmetic  4.22 us (3%)
    ppermute x6, waiting for transfers between devices, across(): return lax.ppermute(v, 'gy', [(i, i ^ mask) for i in range(nz)])  35 us
    ppermute x27, waiting for transfers between devices, swap(): return lax.ppermute(v, 'gx', [(i, i ^ mask) for i in range(nx)])  33.3 us
    ppermute x27, starting transfers between devices, swap(): return lax.ppermute(v, 'gx', [(i, i ^ mask) for i in range(nx)])  25.8 us
    pallas_call x3, Pallas kernels, gate_up(): pl.pallas_call(kernel if all(held) else deep, grid=(n,), in_specs=[pl.Blo...  20.2 us
    ppermute x6, starting transfers between devices, across(): return lax.ppermute(v, 'gy', [(i, i ^ mask) for i in range(nz)])  12.1 us
    pallas_call x1, Pallas kernels, fetch(): pl.pallas_call(kernel, in_specs=[pl.BlockSpec(memory_space=pl.ANY)] * len...  12 us
    pallas_call x3, Pallas kernels, down(): pl.pallas_call(kernel, grid_spec=pltpu.PrefetchScalarGridSpec(num_scalar_...  10.5 us
    pallas_call x1, Pallas kernels, fetch_rows(): pl.pallas_call(kernel, in_specs=[pl.BlockSpec(memory_space=pl.ANY)], out_...  8.78 us
  transfers between devices with their start and end apart: 33, of which 17 were waited for; matrix products, arithmetic and copies ran while one was open for 2% of the time, Pallas kernels for 26%

profile of v4, /device:TPU:0, one launch (start us, length us, event | category | flops | bytes accessed | tf_op | source)
XLA Modules:
  0.0 163.9 jit_solution(8999682662256231461)
XLA Ops:
  0.0 3.1 %collective-permute-start = (bf16[64,2048]{1,0:T(8,128)(2,1)}, bf16[64,2048]{1,0:T(8,128)(2,1)S(1)}, u32[]{:S(2)}, u32[]{:S(2)}) collective-permute-start(bf16[64,2048]{1,0:T(8,128)(2,1)} %refs_0_.2), channel_id=1, source_target_pairs={{0,1},{1,0},{2,3},{3,2},{4,5},{5,4},{6,7},{7,6},{8,9},{9,8},{10,11... | collective-permute-start | bytes 786440 | tf_op jit(solution)/shard_map/ppermute | solution.py:232
  3.1 2.6 %collective-permute-start.1 = (bf16[64,2048]{1,0:T(8,128)(2,1)}, bf16[64,2048]{1,0:T(8,128)(2,1)S(1)}, u32[]{:S(2)}, u32[]{:S(2)}) collective-permute-start(bf16[64,2048]{1,0:T(8,128)(2,1)} %refs_0_.2), channel_id=1, source_target_pairs={{0,2},{1,3},{2,0},{3,1},{4,6},{5,7},{6,4},{7,5},{8,10},{9,11},{10,... | collective-permute-start | bytes 786440 | tf_op jit(solution)/shard_map/ppermute | solution.py:232
  5.6 8.8 %collective-permute-done.refs_1_ = bf16[64,2048]{1,0:T(8,128)(2,1)S(1)} collective-permute-done((bf16[64,2048]{1,0:T(8,128)(2,1)}, bf16[64,2048]{1,0:T(8,128)(2,1)S(1)}, u32[]{:S(2)}, u32[]{:S(2)}) %collective-permute-start) | collective-permute-done | bytes 262176 | tf_op jit(solution)/shard_map/ppermute | solution.py:232
  14.4 10.1 %collective-permute-done.1.refs_2_ = bf16[64,2048]{1,0:T(8,128)(2,1)S(1)} collective-permute-done((bf16[64,2048]{1,0:T(8,128)(2,1)}, bf16[64,2048]{1,0:T(8,128)(2,1)S(1)}, u32[]{:S(2)}, u32[]{:S(2)}) %collective-permute-start.1) | collective-permute-done | bytes 262176 | tf_op jit(solution)/shard_map/ppermute | solution.py:232
  25.7 8.3 %shard_map.50 = (f32[2,128,2048]{2,1,0:T(8,128)S(1)}, f32[2,128,2048]{2,1,0:T(8,128)}) custom-call(bf16[256,2048]{1,0:T(8,128)(2,1)S(1)} %shard_map.46.x, bf16[2048,6656]{1,0:T(8,128)(2,1)} %g.1, bf16[2048,6656]{1,0:T(8,128)(2,1)} %u.1), custom_call_target="tpu_custom_call" | custom-call | flops 4294967296 | bytes 22020096 | tf_op jit(solution)/shard_map/pallas_call | solution.py:134
  34.1 12.0 %shard_map.47 = (bf16[2048,2048]{1,0:T(8,128)(2,1)S(1)}, bf16[2048,2048]{1,0:T(8,128)(2,1)S(1)}, bf16[2048,2560]{1,0:T(8,128)(2,1)S(1)}, bf16[2048,2560]{1,0:T(8,128)(2,1)S(1)}) custom-call(bf16[2048,6656]{1,0:T(8,128)(2,1)} %g.1, bf16[2048,6656]{1,0:T(8,128)(2,1)} %u.1), custom_call_target="tpu_custom_call" | custom-call | bytes 54525952 | tf_op jit(solution)/shard_map/pallas_call | solution.py:86
  46.1 5.3 %shard_map.48 = (f32[2,128,2048]{2,1,0:T(8,128)S(1)}, f32[2,128,2048]{2,1,0:T(8,128)S(1)}) custom-call(bf16[256,2048]{1,0:T(8,128)(2,1)S(1)} %shard_map.46.x, bf16[2048,2048]{1,0:T(8,128)(2,1)S(1)} %get-tuple-element.22.g, bf16[2048,2048]{1,0:T(8,128)(2,1)S(1)} %get-tuple-element.23.u), custom_call_target="tpu_custom_call" | custom-call | flops 4294967296 | bytes 22020096 | tf_op jit(solution)/shard_map/pallas_call | solution.py:134
  51.9 6.5 %shard_map.49 = (f32[2,128,2560]{2,1,0:T(8,128)S(1)}, f32[2,128,2560]{2,1,0:T(8,128)S(1)}) custom-call(bf16[256,2048]{1,0:T(8,128)(2,1)S(1)} %shard_map.46.x, bf16[2048,2560]{1,0:T(8,128)(2,1)S(1)} %get-tuple-element.26.g, bf16[2048,2560]{1,0:T(8,128)(2,1)S(1)} %get-tuple-element.27.u), custom_call_target="tpu_custom_call" | custom-call | flops 5368709120 | bytes 27262976 | tf_op jit(solution)/shard_map/pallas_call | solution.py:134
  59.0 1.8 %slice_add_fusion.2 = (f32[2,64,2048]{2,1,0:T(8,128)S(1)}, f32[2,64,2048]{2,1,0:T(8,128)S(1)}) fusion(f32[2,128,2048]{2,1,0:T(8,128)} %collective-permute-done.3, f32[2,128,2048]{2,1,0:T(8,128)S(1)} %get-tuple-element.24), kind=kLoop, calls=%fused_computation.2 | loop fusion | flops 524288 | bytes 6291456 | tf_op jit(solution)/shard_map/add | solution.py:258
  60.9 1.6 collective-permute-start.10
  65.2 5.0 %collective-permute-done.10 = bf16[2,32,2048]{2,1,0:T(8,128)(2,1)S(1)} collective-permute-done((bf16[2,32,2048]{2,1,0:T(8,128)(2,1)S(1)}, bf16[2,32,2048]{2,1,0:T(8,128)(2,1)S(1)}, u32[]{:S(2)}, u32[]{:S(2)}) %collective-permute-start.10) | collective-permute-done | bytes 262176 | tf_op jit(solution)/shard_map/ppermute | solution.py:229
  70.3 1.6 collective-permute-start.11
  71.8 3.5 %collective-permute-done.4 = bf16[2,32,2048]{2,1,0:T(8,128)(2,1)S(1)} collective-permute-done((bf16[2,32,2048]{2,1,0:T(8,128)(2,1)S(1)}, bf16[2,32,2048]{2,1,0:T(8,128)(2,1)S(1)}, u32[]{:S(2)}, u32[]{:S(2)}) %collective-permute-start.4) | collective-permute-done | bytes 262176 | tf_op jit(solution)/shard_map/ppermute | solution.py:229
  75.4 1.6 collective-permute-start.5
  78.0 1.6 collective-permute-start.25
  80.3 3.0 %collective-permute-done.25 = bf16[2,16,2048]{2,1,0:T(8,128)(2,1)S(1)} collective-permute-done((bf16[2,16,2048]{2,1,0:T(8,128)(2,1)S(1)}, bf16[2,16,2048]{2,1,0:T(8,128)(2,1)S(1)}, u32[]{:S(2)}, u32[]{:S(2)}) %collective-permute-start.25) | collective-permute-done | bytes 131104 | tf_op jit(solution)/shard_map/ppermute | solution.py:229
  83.3 2.3 %collective-permute-start.28 = (bf16[16,2048]{1,0:T(8,128)(2,1)S(1)}, bf16[16,2048]{1,0:T(8,128)(2,1)S(1)}, u32[]{:S(2)}, u32[]{:S(2)}) collective-permute-start(bf16[16,2048]{1,0:T(8,128)(2,1)S(1)} %fusion.23), channel_id=1, source_target_pairs={{0,24},{4,28},{8,16},{12,20},{16,8},{20,12},{24,0},{28,4},{1,25},{... | collective-permute-start | bytes 196616 | tf_op jit(solution)/shard_map/ppermute | solution.py:229
  89.6 4.4 %collective-permute-done.7 = bf16[2,32,2560]{2,1,0:T(8,128)(2,1)S(1)} collective-permute-done((bf16[2,32,2560]{2,1,0:T(8,128)(2,1)S(1)}, bf16[2,32,2560]{2,1,0:T(8,128)(2,1)S(1)}, u32[]{:S(2)}, u32[]{:S(2)}) %collective-permute-start.7) | collective-permute-done | bytes 327712 | tf_op jit(solution)/shard_map/ppermute | solution.py:229
  94.0 1.6 collective-permute-start.8
  95.6 1.5 collective-permute-done.16
  99.6 2.0 %collective-permute-start.14 = (bf16[16,6656]{1,0:T(8,128)(2,1)S(1)}, bf16[16,6656]{1,0:T(8,128)(2,1)S(1)}, u32[]{:S(2)}, u32[]{:S(2)}) collective-permute-start(bf16[16,6656]{1,0:T(8,128)(2,1)S(1)} %pad_maximum_fusion.3), channel_id=1, source_target_pairs={{0,24},{4,28},{8,16},{12,20},{16,8},{20,12},{24,0},{28,4},{1,25},{... | collective-permute-start | bytes 638984 | tf_op jit(solution)/shard_map/ppermute | solution.py:229
  102.4 2.0 %collective-permute-done.17 = bf16[2,16,2560]{2,1,0:T(8,128)(2,1)S(1)} collective-permute-done((bf16[2,16,2560]{2,1,0:T(8,128)(2,1)S(1)}, bf16[2,16,2560]{2,1,0:T(8,128)(2,1)S(1)}, u32[]{:S(2)}, u32[]{:S(2)}) %collective-permute-start.17) | collective-permute-done | bytes 163872 | tf_op jit(solution)/shard_map/ppermute | solution.py:229
  105.5 4.4 %collective-permute-done.14 = bf16[16,6656]{1,0:T(8,128)(2,1)S(1)} collective-permute-done((bf16[16,6656]{1,0:T(8,128)(2,1)S(1)}, bf16[16,6656]{1,0:T(8,128)(2,1)S(1)}, u32[]{:S(2)}, u32[]{:S(2)}) %collective-permute-start.14) | collective-permute-done | bytes 213024 | tf_op jit(solution)/shard_map/ppermute | solution.py:229
  114.6 2.2 %collective-permute-done.22 = bf16[16,4608]{1,0:T(8,128)(2,1)S(1)} collective-permute-done((bf16[16,4608]{1,0:T(8,128)(2,1)S(1)}, bf16[16,4608]{1,0:T(8,128)(2,1)S(1)}, u32[]{:S(2)}, u32[]{:S(2)}) %collective-permute-start.22) | collective-permute-done | bytes 147488 | tf_op jit(solution)/shard_map/ppermute | solution.py:229
  118.8 2.2 %collective-permute-done.26 = bf16[16,2048]{1,0:T(8,128)(2,1)S(1)} collective-permute-done((bf16[16,2048]{1,0:T(8,128)(2,1)S(1)}, bf16[16,2048]{1,0:T(8,128)(2,1)S(1)}, u32[]{:S(2)}, u32[]{:S(2)}) %collective-permute-start.26) | collective-permute-done | bytes 65568 | tf_op jit(solution)/shard_map/ppermute | solution.py:229
  121.1 8.8 %shard_map.51 = (bf16[2048,2048]{1,0:T(8,128)(2,1)S(1)}, bf16[2560,2048]{1,0:T(8,128)(2,1)S(1)}, bf16[2048,2048]{1,0:T(8,128)(2,1)S(1)}) custom-call(bf16[6656,2048]{1,0:T(8,128)(2,1)} %w.1), custom_call_target="tpu_custom_call" | custom-call | bytes 54525952 | tf_op jit(solution)/shard_map/pallas_call | solution.py:166
  129.9 2.0 %shard_map.53.refs_4_ = f32[128,2048]{1,0:T(8,128)S(1)} custom-call(s32[1]{0:T(128)} %bitcast.me_ref, bf16[64,2048]{1,0:T(8,128)(2,1)S(1)} %pad_maximum_fusion.2.refs_0_, bf16[64,2048]{1,0:T(8,128)(2,1)S(1)} %collective-permute-done.29.refs_1_, bf16[2048,2048]{1,0:T(8,128)(2,1)S(1)} %get-tuple-element.32.refs_2_), custom_call_target="tpu_custom_call" | custom-call | flops 1073741824 | bytes 9961472 | tf_op jit(solution)/shard_map/pallas_call | solution.py:212
  132.0 3.7 %shard_map.54 = (bf16[64,2048]{1,0:T(8,128)(2,1)S(1)}, bf16[64,2048]{1,0:T(8,128)(2,1)S(1)}) custom-call(s32[1]{0:T(128)} %bitcast.me_ref, bf16[64,4608]{1,0:T(8,128)(2,1)S(1)} %pad_maximum_fusion.1.refs_0_, bf16[64,4608]{1,0:T(8,128)(2,1)S(1)} %collective-permute-done.23.refs_1_, bf16[2560,2048]{1,0:T(8,128)(2,1)S(1)} %get-tuple-element.33.refs_3_.refs_2_, ...), custom_call_target="tpu_custom_call" | custom-call | flops 2415919104 | bytes 21102592 | tf_op jit(solution)/shard_map/pallas_call | solution.py:212
  135.7 2.5 %collective-permute-start.31 = (bf16[64,2048]{1,0:T(8,128)(2,1)S(1)}, bf16[64,2048]{1,0:T(8,128)(2,1)S(1)}, u32[]{:S(2)}, u32[]{:S(2)}) collective-permute-start(bf16[64,2048]{1,0:T(8,128)(2,1)S(1)} %get-tuple-element.37), channel_id=1, source_target_pairs={{0,3},{1,2},{2,1},{3,0},{4,7},{5,6},{6,5},{7,4},{8,11},{9,10},{10,... | collective-permute-start | bytes 786440 | tf_op jit(solution)/shard_map/ppermute | solution.py:232
  138.2 3.8 %collective-permute-start.30 = (bf16[64,2048]{1,0:T(8,128)(2,1)S(1)}, bf16[64,2048]{1,0:T(8,128)(2,1)S(1)}, u32[]{:S(2)}, u32[]{:S(2)}) collective-permute-start(bf16[64,2048]{1,0:T(8,128)(2,1)S(1)} %get-tuple-element.36), channel_id=1, source_target_pairs={{0,2},{1,3},{2,0},{3,1},{4,6},{5,7},{6,4},{7,5},{8,10},{9,11},{10,... | collective-permute-start | bytes 786440 | tf_op jit(solution)/shard_map/ppermute | solution.py:232
  142.0 4.8 %shard_map.52 = (f32[64,2048]{1,0:T(8,128)S(1)}, bf16[64,2048]{1,0:T(8,128)(2,1)S(1)}) custom-call(s32[1]{0:T(128)} %bitcast.me_ref, bf16[64,6656]{1,0:T(8,128)(2,1)S(1)} %pad_maximum_fusion.refs_0_, bf16[64,6656]{1,0:T(8,128)(2,1)S(1)} %collective-permute-done.15.refs_1_, bf16[2048,2048]{1,0:T(8,128)(2,1)S(1)} %get-tuple-element.32.refs_2_, ...), custom_call_target="tpu_custom_call" | custom-call | flops 3489660928 | bytes 30015488 | tf_op jit(solution)/shard_map/pallas_call | solution.py:212
  147.0 16.1 %collective-permute-done.30 = bf16[64,2048]{1,0:T(8,128)(2,1)S(1)} collective-permute-done((bf16[64,2048]{1,0:T(8,128)(2,1)S(1)}, bf16[64,2048]{1,0:T(8,128)(2,1)S(1)}, u32[]{:S(2)}, u32[]{:S(2)}) %collective-permute-start.30) | collective-permute-done | bytes 262176 | tf_op jit(solution)/shard_map/ppermute | solution.py:232
  (87 shorter events, 22.8 us)
Async XLA Ops:
  0.0 14.4 %collective-permute-start = (bf16[64,2048]{1,0:T(8,128)(2,1)}, bf16[64,2048]{1,0:T(8,128)(2,1)S(1)}, u32[]{:S(2)}, u32[]{:S(2)}) collective-permute-start(bf16[64,2048]{1,0:T(8,128)(2,1)} %refs_0_.2), channel_id=1, source_target_pairs={{0,1},{1,0},{2,3},{3,2},{4,5},{5,4},{6,7},{7,6},{8,9},{9,8},{10,11... | collective-permute-start | bytes 786440 | tf_op jit(solution)/shard_map/ppermute | solution.py:232
  3.1 21.5 %collective-permute-start.1 = (bf16[64,2048]{1,0:T(8,128)(2,1)}, bf16[64,2048]{1,0:T(8,128)(2,1)S(1)}, u32[]{:S(2)}, u32[]{:S(2)}) collective-permute-start(bf16[64,2048]{1,0:T(8,128)(2,1)} %refs_0_.2), channel_id=1, source_target_pairs={{0,2},{1,3},{2,0},{3,1},{4,6},{5,7},{6,4},{7,5},{8,10},{9,11},{10,... | collective-permute-start | bytes 786440 | tf_op jit(solution)/shard_map/ppermute | solution.py:232
  5.6 18.9 %collective-permute-start.2 = (bf16[64,2048]{1,0:T(8,128)(2,1)}, bf16[64,2048]{1,0:T(8,128)(2,1)S(1)}, u32[]{:S(2)}, u32[]{:S(2)}) collective-permute-start(bf16[64,2048]{1,0:T(8,128)(2,1)} %refs_0_.2), channel_id=1, source_target_pairs={{0,3},{1,2},{2,1},{3,0},{4,7},{5,6},{6,5},{7,4},{8,11},{9,10},{10,... | collective-permute-start | bytes 786440 | tf_op jit(solution)/shard_map/ppermute | solution.py:232
  34.0 24.6 %collective-permute-start.9 = (f32[2,128,2048]{2,1,0:T(8,128)}, f32[2,128,2048]{2,1,0:T(8,128)S(1)}, u32[]{:S(2)}, u32[]{:S(2)}) collective-permute-start(f32[2,128,2048]{2,1,0:T(8,128)} %get-tuple-element.31), channel_id=1, source_target_pairs={{0,4},{4,0},{8,12},{12,8},{16,20},{20,16},{24,28},{28,24},{1,5},{5... | collective-permute-start | bytes 6291464 | tf_op jit(solution)/shard_map/ppermute | solution.py:229
  51.4 7.6 %collective-permute-start.3 = (f32[2,128,2048]{2,1,0:T(8,128)S(1)}, f32[2,128,2048]{2,1,0:T(8,128)}, u32[]{:S(2)}, u32[]{:S(2)}) collective-permute-start(f32[2,128,2048]{2,1,0:T(8,128)S(1)} %get-tuple-element.25), channel_id=1, source_target_pairs={{0,4},{4,0},{8,12},{12,8},{16,20},{20,16},{24,28},{28,24},{1,5},{5... | collective-permute-start | bytes 6291464 | tf_op jit(solution)/shard_map/ppermute | solution.py:229
  58.5 27.9 %collective-permute-start.6 = (f32[2,128,2560]{2,1,0:T(8,128)S(1)}, f32[2,128,2560]{2,1,0:T(8,128)S(1)}, u32[]{:S(2)}, u32[]{:S(2)}) collective-permute-start(f32[2,128,2560]{2,1,0:T(8,128)S(1)} %get-tuple-element.29), channel_id=1, source_target_pairs={{0,4},{4,0},{8,12},{12,8},{16,20},{20,16},{24,28},{28,24},{1,5},{5... | collective-permute-start | bytes 7864328 | tf_op jit(solution)/shard_map/ppermute | solution.py:229
  60.9 9.2 %collective-permute-start.10 = (bf16[2,32,2048]{2,1,0:T(8,128)(2,1)S(1)}, bf16[2,32,2048]{2,1,0:T(8,128)(2,1)S(1)}, u32[]{:S(2)}, u32[]{:S(2)}) collective-permute-start(bf16[2,32,2048]{2,1,0:T(8,128)(2,1)S(1)} %fusion.7), channel_id=1, source_target_pairs={{0,16},{4,20},{8,24},{12,28},{16,0},{20,4},{24,8},{28,12},{1,17},{... | collective-permute-start | bytes 786440 | tf_op jit(solution)/shard_map/ppermute | solution.py:229
  62.6 12.8 %collective-permute-start.4 = (bf16[2,32,2048]{2,1,0:T(8,128)(2,1)S(1)}, bf16[2,32,2048]{2,1,0:T(8,128)(2,1)S(1)}, u32[]{:S(2)}, u32[]{:S(2)}) collective-permute-start(bf16[2,32,2048]{2,1,0:T(8,128)(2,1)S(1)} %fusion.6), channel_id=1, source_target_pairs={{0,16},{4,20},{8,24},{12,28},{16,0},{20,4},{24,8},{28,12},{1,17},{... | collective-permute-start | bytes 786440 | tf_op jit(solution)/shard_map/ppermute | solution.py:229
  63.1 16.5 %collective-permute-start.18 = (bf16[2,32,2048]{2,1,0:T(8,128)(2,1)S(1)}, bf16[2,32,2048]{2,1,0:T(8,128)(2,1)S(1)}, u32[]{:S(2)}, u32[]{:S(2)}) collective-permute-start(bf16[2,32,2048]{2,1,0:T(8,128)(2,1)S(1)} %bitcast.161), channel_id=1, source_target_pairs={{0,8},{4,12},{8,0},{12,4},{16,24},{20,28},{24,16},{28,20},{1,9},{5... | collective-permute-start | bytes 786440 | tf_op jit(solution)/shard_map/ppermute | solution.py:229
  64.6 13.3 %collective-permute-start.24 = (bf16[2,32,2048]{2,1,0:T(8,128)(2,1)S(1)}, bf16[2,32,2048]{2,1,0:T(8,128)(2,1)S(1)}, u32[]{:S(2)}, u32[]{:S(2)}) collective-permute-start(bf16[2,32,2048]{2,1,0:T(8,128)(2,1)S(1)} %bitcast.162), channel_id=1, source_target_pairs={{0,8},{4,12},{8,0},{12,4},{16,24},{20,28},{24,16},{28,20},{1,9},{5... | collective-permute-start | bytes 786440 | tf_op jit(solution)/shard_map/ppermute | solution.py:229
  70.3 15.4 %collective-permute-start.11 = (bf16[2,16,2048]{2,1,0:T(8,128)(2,1)S(1)}, bf16[2,16,2048]{2,1,0:T(8,128)(2,1)S(1)}, u32[]{:S(2)}, u32[]{:S(2)}) collective-permute-start(bf16[2,16,2048]{2,1,0:T(8,128)(2,1)S(1)} %fusion.19), channel_id=1, source_target_pairs={{0,8},{4,12},{8,0},{12,4},{16,24},{20,28},{24,16},{28,20},{1,9},{5... | collective-permute-start | bytes 393224 | tf_op jit(solution)/shard_map/ppermute | solution.py:229
  75.4 10.9 %collective-permute-start.5 = (bf16[2,16,2048]{2,1,0:T(8,128)(2,1)S(1)}, bf16[2,16,2048]{2,1,0:T(8,128)(2,1)S(1)}, u32[]{:S(2)}, u32[]{:S(2)}) collective-permute-start(bf16[2,16,2048]{2,1,0:T(8,128)(2,1)S(1)} %fusion.18), channel_id=1, source_target_pairs={{0,8},{4,12},{8,0},{12,4},{16,24},{20,28},{24,16},{28,20},{1,9},{5... | collective-permute-start | bytes 393224 | tf_op jit(solution)/shard_map/ppermute | solution.py:229
  78.0 5.2 %collective-permute-start.25 = (bf16[2,16,2048]{2,1,0:T(8,128)(2,1)S(1)}, bf16[2,16,2048]{2,1,0:T(8,128)(2,1)S(1)}, u32[]{:S(2)}, u32[]{:S(2)}) collective-permute-start(bf16[2,16,2048]{2,1,0:T(8,128)(2,1)S(1)} %fusion.21), channel_id=1, source_target_pairs={{0,16},{4,20},{8,24},{12,28},{16,0},{20,4},{24,8},{28,12},{1,17},{... | collective-permute-start | bytes 393224 | tf_op jit(solution)/shard_map/ppermute | solution.py:229
  79.7 6.7 %collective-permute-start.19 = (bf16[2,16,2048]{2,1,0:T(8,128)(2,1)S(1)}, bf16[2,16,2048]{2,1,0:T(8,128)(2,1)S(1)}, u32[]{:S(2)}, u32[]{:S(2)}) collective-permute-start(bf16[2,16,2048]{2,1,0:T(8,128)(2,1)S(1)} %fusion.20), channel_id=1, source_target_pairs={{0,16},{4,20},{8,24},{12,28},{16,0},{20,4},{24,8},{28,12},{1,17},{... | collective-permute-start | bytes 393224 | tf_op jit(solution)/shard_map/ppermute | solution.py:229
  83.3 35.4 %collective-permute-start.28 = (bf16[16,2048]{1,0:T(8,128)(2,1)S(1)}, bf16[16,2048]{1,0:T(8,128)(2,1)S(1)}, u32[]{:S(2)}, u32[]{:S(2)}) collective-permute-start(bf16[16,2048]{1,0:T(8,128)(2,1)S(1)} %fusion.23), channel_id=1, source_target_pairs={{0,24},{4,28},{8,16},{12,20},{16,8},{20,12},{24,0},{28,4},{1,25},{... | collective-permute-start | bytes 196616 | tf_op jit(solution)/shard_map/ppermute | solution.py:229
  85.7 33.1 %collective-permute-start.27 = (bf16[16,2048]{1,0:T(8,128)(2,1)S(1)}, bf16[16,2048]{1,0:T(8,128)(2,1)S(1)}, u32[]{:S(2)}, u32[]{:S(2)}) collective-permute-start(bf16[16,2048]{1,0:T(8,128)(2,1)S(1)} %fusion.23), channel_id=1, source_target_pairs={{0,16},{4,20},{8,24},{12,28},{16,0},{20,4},{24,8},{28,12},{1,17},{... | collective-permute-start | bytes 196616 | tf_op jit(solution)/shard_map/ppermute | solution.py:229
  86.8 7.1 %collective-permute-start.7 = (bf16[2,32,2560]{2,1,0:T(8,128)(2,1)S(1)}, bf16[2,32,2560]{2,1,0:T(8,128)(2,1)S(1)}, u32[]{:S(2)}, u32[]{:S(2)}) collective-permute-start(bf16[2,32,2560]{2,1,0:T(8,128)(2,1)S(1)} %bitcast.160), channel_id=1, source_target_pairs={{0,8},{4,12},{8,0},{12,4},{16,24},{20,28},{24,16},{28,20},{1,9},{5... | collective-permute-start | bytes 983048 | tf_op jit(solution)/shard_map/ppermute | solution.py:229
  88.2 8.9 %collective-permute-start.16 = (bf16[2,32,2560]{2,1,0:T(8,128)(2,1)S(1)}, bf16[2,32,2560]{2,1,0:T(8,128)(2,1)S(1)}, u32[]{:S(2)}, u32[]{:S(2)}) collective-permute-start(bf16[2,32,2560]{2,1,0:T(8,128)(2,1)S(1)} %fusion.3), channel_id=1, source_target_pairs={{0,16},{4,20},{8,24},{12,28},{16,0},{20,4},{24,8},{28,12},{1,17},{... | collective-permute-start | bytes 983048 | tf_op jit(solution)/shard_map/ppermute | solution.py:229
  94.0 5.4 %collective-permute-start.8 = (bf16[2,16,2560]{2,1,0:T(8,128)(2,1)S(1)}, bf16[2,16,2560]{2,1,0:T(8,128)(2,1)S(1)}, u32[]{:S(2)}, u32[]{:S(2)}) collective-permute-start(bf16[2,16,2560]{2,1,0:T(8,128)(2,1)S(1)} %fusion.12), channel_id=1, source_target_pairs={{0,16},{4,20},{8,24},{12,28},{16,0},{20,4},{24,8},{28,12},{1,17},{... | collective-permute-start | bytes 491528 | tf_op jit(solution)/shard_map/ppermute | solution.py:229
  97.2 7.1 %collective-permute-start.17 = (bf16[2,16,2560]{2,1,0:T(8,128)(2,1)S(1)}, bf16[2,16,2560]{2,1,0:T(8,128)(2,1)S(1)}, u32[]{:S(2)}, u32[]{:S(2)}) collective-permute-start(bf16[2,16,2560]{2,1,0:T(8,128)(2,1)S(1)} %fusion.13), channel_id=1, source_target_pairs={{0,8},{4,12},{8,0},{12,4},{16,24},{20,28},{24,16},{28,20},{1,9},{5... | collective-permute-start | bytes 491528 | tf_op jit(solution)/shard_map/ppermute | solution.py:229
  99.6 10.3 %collective-permute-start.14 = (bf16[16,6656]{1,0:T(8,128)(2,1)S(1)}, bf16[16,6656]{1,0:T(8,128)(2,1)S(1)}, u32[]{:S(2)}, u32[]{:S(2)}) collective-permute-start(bf16[16,6656]{1,0:T(8,128)(2,1)S(1)} %pad_maximum_fusion.3), channel_id=1, source_target_pairs={{0,24},{4,28},{8,16},{12,20},{16,8},{20,12},{24,0},{28,4},{1,25},{... | collective-permute-start | bytes 638984 | tf_op jit(solution)/shard_map/ppermute | solution.py:229
  101.6 10.4 %collective-permute-start.13 = (bf16[16,6656]{1,0:T(8,128)(2,1)S(1)}, bf16[16,6656]{1,0:T(8,128)(2,1)S(1)}, u32[]{:S(2)}, u32[]{:S(2)}) collective-permute-start(bf16[16,6656]{1,0:T(8,128)(2,1)S(1)} %pad_maximum_fusion.3), channel_id=1, source_target_pairs={{0,16},{4,20},{8,24},{12,28},{16,0},{20,4},{24,8},{28,12},{1,17},{... | collective-permute-start | bytes 638984 | tf_op jit(solution)/shard_map/ppermute | solution.py:229
  104.4 9.1 %collective-permute-start.12 = (bf16[16,6656]{1,0:T(8,128)(2,1)S(1)}, bf16[16,6656]{1,0:T(8,128)(2,1)S(1)}, u32[]{:S(2)}, u32[]{:S(2)}) collective-permute-start(bf16[16,6656]{1,0:T(8,128)(2,1)S(1)} %pad_maximum_fusion.3), channel_id=1, source_target_pairs={{0,8},{4,12},{8,0},{12,4},{16,24},{20,28},{24,16},{28,20},{1,9},{5... | collective-permute-start | bytes 638984 | tf_op jit(solution)/shard_map/ppermute | solution.py:229
  109.9 6.9 %collective-permute-start.22 = (bf16[16,4608]{1,0:T(8,128)(2,1)S(1)}, bf16[16,4608]{1,0:T(8,128)(2,1)S(1)}, u32[]{:S(2)}, u32[]{:S(2)}) collective-permute-start(bf16[16,4608]{1,0:T(8,128)(2,1)S(1)} %pad_maximum_fusion.4), channel_id=1, source_target_pairs={{0,24},{4,28},{8,16},{12,20},{16,8},{20,12},{24,0},{28,4},{1,25},{... | collective-permute-start | bytes 442376 | tf_op jit(solution)/shard_map/ppermute | solution.py:229
  112.0 5.9 %collective-permute-start.21 = (bf16[16,4608]{1,0:T(8,128)(2,1)S(1)}, bf16[16,4608]{1,0:T(8,128)(2,1)S(1)}, u32[]{:S(2)}, u32[]{:S(2)}) collective-permute-start(bf16[16,4608]{1,0:T(8,128)(2,1)S(1)} %pad_maximum_fusion.4), channel_id=1, source_target_pairs={{0,16},{4,20},{8,24},{12,28},{16,0},{20,4},{24,8},{28,12},{1,17},{... | collective-permute-start | bytes 442376 | tf_op jit(solution)/shard_map/ppermute | solution.py:229
  113.5 5.1 %collective-permute-start.20 = (bf16[16,4608]{1,0:T(8,128)(2,1)S(1)}, bf16[16,4608]{1,0:T(8,128)(2,1)S(1)}, u32[]{:S(2)}, u32[]{:S(2)}) collective-permute-start(bf16[16,4608]{1,0:T(8,128)(2,1)S(1)} %pad_maximum_fusion.4), channel_id=1, source_target_pairs={{0,8},{4,12},{8,0},{12,4},{16,24},{20,28},{24,16},{28,20},{1,9},{5... | collective-permute-start | bytes 442376 | tf_op jit(solution)/shard_map/ppermute | solution.py:229
  117.8 24.2 %collective-permute-start.15 = (bf16[64,6656]{1,0:T(8,128)(2,1)S(1)}, bf16[64,6656]{1,0:T(8,128)(2,1)S(1)}, u32[]{:S(2)}, u32[]{:S(2)}) collective-permute-start(bf16[64,6656]{1,0:T(8,128)(2,1)S(1)} %pad_maximum_fusion.refs_0_), channel_id=1, source_target_pairs={{0,4},{4,0},{8,12},{12,8},{16,20},{20,16},{24,28},{28,24},{1,5},{5... | collective-permute-start | bytes 2555912 | tf_op jit(solution)/shard_map/ppermute | solution.py:229
  118.7 13.3 %collective-permute-start.23 = (bf16[64,4608]{1,0:T(8,128)(2,1)S(1)}, bf16[64,4608]{1,0:T(8,128)(2,1)S(1)}, u32[]{:S(2)}, u32[]{:S(2)}) collective-permute-start(bf16[64,4608]{1,0:T(8,128)(2,1)S(1)} %pad_maximum_fusion.1.refs_0_), channel_id=1, source_target_pairs={{0,4},{4,0},{8,12},{12,8},{16,20},{20,16},{24,28},{28,24},{1,5},{5... | collective-permute-start | bytes 1769480 | tf_op jit(solution)/shard_map/ppermute | solution.py:229
  121.0 8.9 %collective-permute-start.29 = (bf16[64,2048]{1,0:T(8,128)(2,1)S(1)}, bf16[64,2048]{1,0:T(8,128)(2,1)S(1)}, u32[]{:S(2)}, u32[]{:S(2)}) collective-permute-start(bf16[64,2048]{1,0:T(8,128)(2,1)S(1)} %pad_maximum_fusion.2.refs_0_), channel_id=1, source_target_pairs={{0,4},{4,0},{8,12},{12,8},{16,20},{20,16},{24,28},{28,24},{1,5},{5... | collective-permute-start | bytes 786440 | tf_op jit(solution)/shard_map/ppermute | solution.py:229
  135.7 11.3 %collective-permute-start.31 = (bf16[64,2048]{1,0:T(8,128)(2,1)S(1)}, bf16[64,2048]{1,0:T(8,128)(2,1)S(1)}, u32[]{:S(2)}, u32[]{:S(2)}) collective-permute-start(bf16[64,2048]{1,0:T(8,128)(2,1)S(1)} %get-tuple-element.37), channel_id=1, source_target_pairs={{0,3},{1,2},{2,1},{3,0},{4,7},{5,6},{6,5},{7,4},{8,11},{9,10},{10,... | collective-permute-start | bytes 786440 | tf_op jit(solution)/shard_map/ppermute | solution.py:232
  138.2 24.9 %collective-permute-start.30 = (bf16[64,2048]{1,0:T(8,128)(2,1)S(1)}, bf16[64,2048]{1,0:T(8,128)(2,1)S(1)}, u32[]{:S(2)}, u32[]{:S(2)}) collective-permute-start(bf16[64,2048]{1,0:T(8,128)(2,1)S(1)} %get-tuple-element.36), channel_id=1, source_target_pairs={{0,2},{1,3},{2,0},{3,1},{4,6},{5,7},{6,4},{7,5},{8,10},{9,11},{10,... | collective-permute-start | bytes 786440 | tf_op jit(solution)/shard_map/ppermute | solution.py:232
  146.8 16.3 %collective-permute-start.32 = (bf16[64,2048]{1,0:T(8,128)(2,1)S(1)}, bf16[64,2048]{1,0:T(8,128)(2,1)S(1)}, u32[]{:S(2)}, u32[]{:S(2)}) collective-permute-start(bf16[64,2048]{1,0:T(8,128)(2,1)S(1)} %get-tuple-element.38), channel_id=1, source_target_pairs={{0,1},{1,0},{2,3},{3,2},{4,5},{5,4},{6,7},{7,6},{8,9},{9,8},{10,11... | collective-permute-start | bytes 786440 | tf_op jit(solution)/shard_map/ppermute | solution.py:232
  (2 other events, 5.2 us)
